TPU v7x, 512 devices: a whole 4x4x16 slice. The times are simulated.
512 devices in a mesh: angle: 128 (over y, x_hi, z), tile: 4 (over x_lo, core).
Axes of the slice: x: 4 (x_hi: 2, x_lo: 2; x = x_hi * 2 + x_lo), y: 4, z: 16, core: 2. Of those that a mesh axis runs over, the one named last changes fastest.
Arguments:
- projection: float32 [2, 128, 1024, 512], P(None, 'angle', 'tile'), may hold values from -5 to 5
- probe: float32 [2, 128, 128], replicated, may hold values from -5 to 5
- amplitude: float32 [128, 16, 128, 128], P('angle', 'tile'), may hold values from 0.4 to 2.2
- pos_row: int32 [128, 16], P('angle', 'tile'), may hold values from 0 to 255
- pos_col: int32 [128, 16], P('angle', 'tile'), may hold values from 0 to 384
- ang_offset: int32 [128], replicated, may hold values from 0 to 124, as said below
- ang_weight: float32 [128, 4], replicated, may hold values from 0.1 to 0.6
- det_offset: int32 [256], replicated, may hold values from 0 to 508, as said below
- det_weight: float32 [256, 4], replicated, may hold values from 0.1 to 0.6
Outputs:
- updated_projection: float32 [2, 128, 1024, 512], P(None, 'angle', 'tile')
- probe_direction: float32 [2, 128, 128], replicated
- volume: float32 [2, 4, 256, 128, 256], P(None, 'tile', 'angle')
Inputs may be any that keep to these rules, and one draw needn't show every extreme that they name: `ang_offset`: regular angle r's band starts within one of r - 1, clipped to the valid range; both ends are reached. `det_offset`: radial sample q's band starts within one of 2 q - 1, clipped to the valid range; both ends are reached.
All inputs are finite; a program needn't handle non-finite values.
Results may differ from a plain program's by a relative error of at most 0.00011.
Values sent between devices are 32-bit elements; how exact they have to be, the bound alone decides.
No kernel may reach another device: no remote copies, remote signals or barrier semaphores. Data moves between devices by JAX's collectives and lax.ppermute only.
A program may use at most 64 MiB of HBM per device.

v0:
```python
import math

import jax
import jax.numpy as jnp
from jax import lax
from jax.sharding import PartitionSpec as P

STEP_SIZE = 0.1
EPSILON = 1e-06
HIGHEST = lax.Precision.HIGHEST


def with_halo(value, sides, width):
    for axis, dim in sides:
        count, length = (lax.axis_size(axis), value.shape[dim])
        up = [(i, (i + 1) % count) for i in range(count - 1)]
        down = [(j, i) for i, j in up]
        last = lax.slice_in_dim(value, length - width, length, axis=dim)
        initial = lax.slice_in_dim(value, 0, width, axis=dim)
        before = lax.ppermute(last, axis, up)
        after = lax.ppermute(initial, axis, down)
        value = jnp.concatenate([before, value, after], axis=dim)
    return value


def passed_along(value, axis, by):
    count = lax.axis_size(axis)
    pairs = [(i, i + by) for i in range(count) if 0 <= i + by < count]
    return lax.ppermute(value, axis, pairs)


def dft_tables(length):
    counter = jnp.arange(length, dtype=jnp.int32)
    product_mod = counter[:, None] * counter[None, :] % length
    angle_table = product_mod.astype(jnp.float32) * (2.0 * math.pi / length)
    norm_scale = 1.0 / math.sqrt(length)
    return (jnp.cos(angle_table) * norm_scale, -jnp.sin(angle_table) * norm_scale)


def transform(values_re, values_im, table_re, table_im):
    left_re = jnp.einsum("ij,bjk->bik", table_re, values_re, precision=HIGHEST) - jnp.einsum(
        "ij,bjk->bik", table_im, values_im, precision=HIGHEST
    )
    left_im = jnp.einsum("ij,bjk->bik", table_re, values_im, precision=HIGHEST) + jnp.einsum(
        "ij,bjk->bik", table_im, values_re, precision=HIGHEST
    )
    right_re = jnp.einsum("bij,jk->bik", left_re, table_re, precision=HIGHEST) - jnp.einsum(
        "bij,jk->bik", left_im, table_im, precision=HIGHEST
    )
    right_im = jnp.einsum("bij,jk->bik", left_re, table_im, precision=HIGHEST) + jnp.einsum(
        "bij,jk->bik", left_im, table_re, precision=HIGHEST
    )
    return (right_re, right_im)


def patch_terms(object_re, object_im, amp_block, probe_re, probe_im, cosine_table, sine_table):
    exit_re = probe_re * object_re - probe_im * object_im
    exit_im = probe_re * object_im + probe_im * object_re
    spec_re, spec_im = transform(exit_re, exit_im, cosine_table, sine_table)
    magnitude = jnp.sqrt(spec_re * spec_re + spec_im * spec_im)
    factor = 1.0 - amp_block / jnp.maximum(magnitude, 1.0)
    back_re, back_im = transform(spec_re * factor, spec_im * factor, cosine_table, -sine_table)
    grad_re = probe_re * back_re + probe_im * back_im
    grad_im = probe_re * back_im - probe_im * back_re
    term_re = jnp.sum(object_re * back_re + object_im * back_im, axis=0)
    term_im = jnp.sum(object_re * back_im - object_im * back_re, axis=0)
    weight_sum = jnp.sum(object_re * object_re + object_im * object_im, axis=0)
    return (grad_re, grad_im, term_re, term_im, weight_sum)


def band_matrix(offset, weight, length):
    columns = jnp.arange(length, dtype=jnp.int32)
    matrix = jnp.zeros((offset.shape[0], length), jnp.float32)
    for band_step in range(weight.shape[1]):
        hits = (columns[None, :] == offset[:, None] + band_step).astype(jnp.float32)
        matrix = matrix + weight[:, band_step : band_step + 1] * hits
    return matrix


def local(
    projection, probe, amplitude, pos_row, pos_col, ang_offset, ang_weight, det_offset, det_weight
):
    patch_side = probe.shape[-1]
    half_rows = patch_side // 2
    tile_rows = projection.shape[2]
    detector = projection.shape[3]
    patch_count = amplitude.shape[1]
    block_size = math.gcd(patch_count, 8)
    block_count = patch_count // block_size
    cosine_table, sine_table = dft_tables(patch_side)
    probe_re = probe[0]
    probe_im = probe[1]
    current = projection[:, 0]
    padded = with_halo(current, (("tile", 1),), half_rows)
    row_blocks = pos_row[0].reshape(block_count, block_size)
    col_blocks = pos_col[0].reshape(block_count, block_size)
    amp_blocks = amplitude[0].reshape(block_count, block_size, patch_side, patch_side)

    def cut_patch(start_row, start_col):
        return lax.dynamic_slice(
            padded, (jnp.int32(0), start_row, start_col), (2, patch_side, patch_side)
        )

    def one_block(carried, inputs):
        row_here, col_here, amp_here = inputs
        pieces = jax.vmap(cut_patch)(row_here, col_here)
        grad_re, grad_im, term_re, term_im, weight_sum = patch_terms(
            pieces[:, 0], pieces[:, 1], amp_here, probe_re, probe_im, cosine_table, sine_table
        )

        def deposit(number, accumulated):
            corner = (jnp.int32(0), row_here[number], col_here[number])
            window = lax.dynamic_slice(accumulated, corner, (2, patch_side, patch_side))
            addend = jnp.stack([grad_re[number], grad_im[number]])
            return lax.dynamic_update_slice(accumulated, window + addend, corner)

        gradient = lax.fori_loop(0, block_size, deposit, carried[0])
        return (
            (gradient, carried[1] + term_re, carried[2] + term_im, carried[3] + weight_sum),
            None,
        )

    zeros_pp = jnp.zeros((patch_side, patch_side), jnp.float32)
    initial = (jnp.zeros_like(padded), zeros_pp, zeros_pp, zeros_pp)
    gradient, probe_acc_re, probe_acc_im, intensity = lax.scan(
        one_block, initial, (row_blocks, col_blocks, amp_blocks)
    )[0]
    inner_rows = gradient[:, half_rows : half_rows + tile_rows]
    upper_rim = gradient[:, :half_rows]
    lower_rim = gradient[:, half_rows + tile_rows :]
    middle = jnp.zeros((2, tile_rows - 2 * half_rows, detector), jnp.float32)
    from_below = passed_along(upper_rim, "tile", -1)
    from_above = passed_along(lower_rim, "tile", 1)
    inner_rows = inner_rows + jnp.concatenate([from_above, middle, from_below], axis=1)
    updated = current - STEP_SIZE * inner_rows
    total_re, total_im, total_den = lax.psum(
        (probe_acc_re, probe_acc_im, intensity), ("angle", "tile")
    )
    norm_scale = lax.rsqrt(total_den + EPSILON)
    direction = jnp.stack([total_re * norm_scale, total_im * norm_scale])
    det_matrix = band_matrix(det_offset, det_weight, detector)
    ang_matrix = band_matrix(ang_offset, ang_weight, ang_weight.shape[0])
    arrived_rows = lax.all_to_all(
        updated[:, None], "angle", split_axis=2, concat_axis=1, tiled=True
    )
    sliced = jnp.einsum("casw,qw->casq", arrived_rows, det_matrix, precision=HIGHEST)
    volume = jnp.einsum("ra,casq->csrq", ang_matrix, sliced, precision=HIGHEST)
    return (updated[:, None], direction, volume[:, None])


def solution(mesh):
    in_specs = (
        P(None, "angle", "tile", None),
        P(),
        P("angle", "tile", None, None),
        P("angle", "tile"),
        P("angle", "tile"),
        P(),
        P(),
        P(),
        P(),
    )
    out_specs = (P(None, "angle", "tile", None), P(), P(None, "tile", "angle", None, None))
    return jax.shard_map(local, mesh=mesh, in_specs=in_specs, out_specs=out_specs, check_vma=False)
```

profile of v0, /device:TPU:1, one launch (start us, length us, event | category | flops | bytes accessed | tf_op | source)
XLA Modules:
  0.0 592.9 jit_solution(8981152005080590323)
XLA Ops:
  7.2 1.2 fusion.177
  8.3 4.5 collective-permute-start
  12.8 5.6 collective-permute-start.1
  19.2 0.9 slice_bitcast_fusion.1
  20.6 1.1 pad_maximum_fusion
  21.7 8.2 %while.25 = (s32[]{:T(128)}, f32[2,384,512]{2,1,0:T(8,128)S(1)}, s32[4,3]{1,0:T(4,128)S(1)}, f32[4,2,128,128]{3,2,0,1:T(8,128)S(1)}, s32[]{:T(128)}) while((s32[]{:T(128)}, f32[2,384,512]{2,1,0:T(8,128)S(1)}, s32[4,3]{1,0:T(4,128)S(1)}, f32[4,2,128,128]{3,2,0,1:T(8,128)S(1)}, s32[]{:T(128)}) %tuple.82), condition=%wide.while_cond, body=%wide.while_body.sunk | while | flops 2 | bytes 262269 | solution.py:100
  22.4 1.4 bitcast_dynamic-update-slice_fusion.2
  24.5 1.4 bitcast_dynamic-update-slice_fusion.2
  26.5 1.4 bitcast_dynamic-update-slice_fusion.2
  28.6 1.4 bitcast_dynamic-update-slice_fusion.2
  30.0 0.8 fusion.62
  30.7 0.8 fusion.3
  33.0 0.8 fusion.58
  33.8 0.8 fusion.2
  35.3 0.8 fusion.34
  41.2 1.6 fusion.20
  43.0 30.8 %while.24 = (s32[]{:T(128)}, f32[2,384,512]{2,1,0:T(8,128)S(1)}, s32[4]{0:T(128)S(1)}, s32[4]{0:T(128)S(1)}, f32[4,128,128]{2,1,0:T(8,128)S(1)}, /*index=5*/f32[...) while((s32[]{:T(128)}, f32[2,384,512]{2,1,0:T(8,128)S(1)}, s32[4]{0:T(128)S(1)}, ...), condition=%wide.region_1.2_spmd, body=%wide.region_0.1_spmd.sunk | while | flops 65544 | bytes 917721 | solution.py:117
  48.2 2.4 dynamic_update_slice.8
  55.9 2.5 dynamic_update_slice.8
  63.6 2.5 dynamic_update_slice.8
  71.3 2.5 dynamic_update_slice.8
  73.9 1.9 collective-permute-start.2
  75.8 2.4 collective-permute-start.3
  78.3 0.8 collective-permute-done.2
  79.1 4.4 collective-permute-done.3
  83.5 1.2 fusion.174
  84.7 1.8 copy.101
  86.5 21.7 %all-to-all-start = ((f32[2,1,256,512]{3,0,1,2:T(2,128)}), f32[2,1,256,512]{3,0,1,2:T(2,128)S(1)}, u32[]{:S(2)}, u32[]{:S(2)}) async-start(f32[2,1,256,512]{3,0,1,2:T(2,128)} %copy.101), calls=%async_computation | async-start | bytes 2097152 | tf_op jit(solution)/shard_map/all_to_all | solution.py:143
  109.1 472.1 %all-reduce.3.cloned.1.call-done = (f32[128,128]{1,0:T(8,128)}, f32[128,128]{1,0:T(8,128)}, f32[128,128]{1,0:T(8,128)}) async-done(((f32[128,128]{1,0:T(8,128)}, f32[128,128]{1,0:T(8,128)}, f32[128,128]{1,0:T(8,128)}), (f32[128,128]{1,0:T(8,128)}, f32[128,128]{1,0:T(8,128)}, f32[128,128]{1,0:T(8,128)})) %all-reduce.3.cloned.1.call-update) | async-done | bytes 196624 | tf_op jit(solution)/shard_map/psum | solution.py:136
  581.2 0.9 multiply_bitcast_fusion.1
  582.8 1.6 fusion.6
  585.1 1.0 copy.105
  (70 shorter events, 19.4 us)
Async XLA Ops:
  7.2 13.5 %copy-start = (f32[2,1,256,512]{3,2,1,0:T(8,128)S(1)}, f32[2,1,256,512]{3,2,1,0:T(8,128)}, u32[]{:S(2)}) copy-start(f32[2,1,256,512]{3,2,1,0:T(8,128)} %param.11) | copy-start | bytes 3145732
  8.3 11.8 %collective-permute-start = (f32[2,64,512]{2,1,0:T(8,128)S(1)}, f32[2,64,512]{2,1,0:T(8,128)S(1)}, u32[]{:S(2)}, u32[]{:S(2)}) collective-permute-start(f32[2,64,512]{2,1,0:T(8,128)S(1)} %get-tuple-element.230), channel_id=1, source_target_pairs={{0,1},{1,2},{2,3},{4,5},{5,6},{6,7},{8,9},{9,10},{10,11},{12,13},{... | collective-permute-start | bytes 786440 | tf_op jit(solution)/shard_map/ppermute | solution.py:20
  12.8 7.8 %collective-permute-start.1 = (f32[2,64,512]{2,1,0:T(8,128)S(1)}, f32[2,64,512]{2,1,0:T(8,128)}, u32[]{:S(2)}, u32[]{:S(2)}) collective-permute-start(f32[2,64,512]{2,1,0:T(8,128)S(1)} %get-tuple-element.231), channel_id=1, source_target_pairs={{1,0},{2,1},{3,2},{5,4},{6,5},{7,6},{9,8},{10,9},{11,10},{13,12},{... | collective-permute-start | bytes 786440 | tf_op jit(solution)/shard_map/ppermute | solution.py:21
  32.2 3.0 copy-start.7
  41.2 1.8 copy-start.5
  41.2 1.8 copy-start.6
  73.9 5.2 collective-permute-start.2
  75.8 7.7 %collective-permute-start.3 = (f32[2,64,512]{2,1,0:T(8,128)S(1)}, f32[2,64,512]{2,1,0:T(8,128)S(1)}, u32[]{:S(2)}, u32[]{:S(2)}) collective-permute-start(f32[2,64,512]{2,1,0:T(8,128)S(1)} %get-tuple-element.229), channel_id=1, source_target_pairs={{1,0},{2,1},{3,2},{5,4},{6,5},{7,6},{9,8},{10,9},{11,10},{13,12},{... | collective-permute-start | bytes 786440 | tf_op jit(solution)/shard_map/ppermute | solution.py:29
  86.5 21.8 %copy-start.3 = (f32[128,4]{0,1:T(4,128)S(1)}, f32[128,4]{0,1:T(4,128)}, u32[]{:S(2)}) copy-start(f32[128,4]{0,1:T(4,128)} %param.17) | copy-start | bytes 6148
  86.5 21.8 %copy-start.4 = (s32[256]{0:T(256)S(1)}, s32[256]{0:T(256)}, u32[]{:S(2)}) copy-start(s32[256]{0:T(256)} %param.18) | copy-start | bytes 3076
  86.5 21.9 %copy-start.1 = (f32[256,4]{0,1:T(4,128)S(1)}, f32[256,4]{0,1:T(4,128)}, u32[]{:S(2)}) copy-start(f32[256,4]{0,1:T(4,128)} %param.19) | copy-start | bytes 12292
  86.5 22.5 %copy-start.2 = (s32[128]{0:T(128)S(1)}, s32[128]{0:T(128)}, u32[]{:S(2)}) copy-start(s32[128]{0:T(128)} %param.16) | copy-start | bytes 1540
  86.5 496.2 %all-to-all-start = ((f32[2,1,256,512]{3,0,1,2:T(2,128)}), f32[2,1,256,512]{3,0,1,2:T(2,128)S(1)}, u32[]{:S(2)}, u32[]{:S(2)}) async-start(f32[2,1,256,512]{3,0,1,2:T(2,128)} %copy.101), calls=%async_computation | async-start | bytes 2097152 | tf_op jit(solution)/shard_map/all_to_all | solution.py:143
  108.3 472.9 %all-reduce.3.cloned.1.call-start = ((), (), s32[]{:S(2)}) async-start(), calls=%async_computation.1 | async-start | bytes 393216 | tf_op jit(solution)/shard_map/psum | solution.py:136
Sparse Core Ops, SparseCore 0:
  115.5 465.6 all-reduce.2
where the time goes:
time: 594 us; the launch traced here: 593 us
  waiting for transfers between devices  478 us (80%)
  starting transfers between devices  36.2 us (6%)
  local copies, waits for them, and re-layouts  28.6 us (5%)
  loops' own time  15.3 us (3%)
  matrix products  15 us (3%)
  between operations  14.4 us (2%)
    psum x1, waiting for transfers between devices, local(): lax.psum((probe_acc_re, probe_acc_im, intensity), ('angle', 'tile'))  472 us
    all_to_all x1, starting transfers between devices, local(): lax.all_to_all(updated[:, None], 'angle', split_axis=2, concat_axis=1, ti...  21.7 us
    another operation x1, loops' own time, one_block(): gradient = lax.fori_loop(0, block_size, deposit, carried[0])  15.1 us
  transfers between devices with their start and end apart: 6, of which 4 were waited for; matrix products, arithmetic and copies ran while one was open for 1% of the time, Pallas kernels for 0%

commit v1 on v0

v1 whole, which is shorter than its diff:
```python
import functools

import jax
import jax.numpy as jnp
import numpy as np
from jax import lax
from jax.experimental import pallas as pl
from jax.experimental.pallas import tpu as pltpu
from jax.sharding import PartitionSpec as P

STEP_SIZE = 0.1
EPSILON = 1e-06
F32 = jnp.float32
BF16 = jnp.bfloat16


def complex_table(length):
    counter = np.arange(length)
    angle = (counter[:, None] * counter[None, :] % length) * (2.0 * np.pi / length)
    re = np.cos(angle) / np.sqrt(length)
    im = -np.sin(angle) / np.sqrt(length)
    table = np.block([[re, -im], [im, re]]).astype(np.float32)
    high = table.astype(BF16)
    low = (table - high.astype(np.float32)).astype(BF16)
    return high, low


def split(value):
    high = value.astype(BF16)
    low = (value - high.astype(F32)).astype(BF16)
    return high, low


def dot3(left, right):
    mul = functools.partial(jnp.dot, preferred_element_type=F32)
    return mul(left[0], right[0]) + (mul(left[0], right[1]) + mul(left[1], right[0]))


def patch_kernel(
    row_ref, col_ref, cur_ref, before_ref, after_ref, probe_ref, amp_ref,
    gh_ref, gl_ref, th_ref, tl_ref,
    own_ref, up_ref, down_ref, term_ref,
    padded, grad, objects, tall, wide,
):
    side = probe_ref.shape[-1]
    half = side // 2
    rows = cur_ref.shape[1]
    lanes = cur_ref.shape[2]
    count = amp_ref.shape[0]
    window = 2 * side
    tall_side = side + 8

    padded[:, :half] = before_ref[...]
    padded[:, half : half + rows] = cur_ref[...]
    padded[:, half + rows :] = after_ref[...]
    grad[...] = jnp.zeros(grad.shape, F32)

    def place(k):
        row = row_ref[0, k]
        col = col_ref[0, k]
        first = lax.div(row, 8)
        base = jnp.minimum(lax.div(col, side), lanes // side - 2)
        where = (
            pl.ds(pl.multiple_of(first * 8, 8), tall_side),
            pl.ds(pl.multiple_of(base * side, side), window),
        )
        return where, row - first * 8, col - base * side

    probe_re = probe_ref[0]
    probe_im = probe_ref[1]
    for k in range(count):
        where, row_shift, col_shift = place(k)
        row_back = lax.rem(tall_side - row_shift, tall_side)
        col_back = lax.rem(window - col_shift, window)
        for c in range(2):
            block = padded[(c,) + where]
            block = pltpu.roll(block, col_back, 1)[:, :side]
            objects[k, c] = pltpu.roll(block, row_back, 0)[:side]
        o_re = objects[k, 0]
        o_im = objects[k, 1]
        here = slice(k * side, (k + 1) * side)
        tall[:side, here] = probe_re * o_re - probe_im * o_im
        tall[side:, here] = probe_re * o_im + probe_im * o_re

    table = (gh_ref[...], gl_ref[...])
    flipped = (th_ref[...], tl_ref[...])

    left = dot3(table, split(tall[...]))
    for k in range(count):
        here = slice(k * side, (k + 1) * side)
        wide[here, :side] = left[:side, here]
        wide[here, side:] = left[side:, here]
    spec = dot3(split(wide[...]), flipped)
    for k in range(count):
        here = slice(k * side, (k + 1) * side)
        s_re = spec[here, :side]
        s_im = spec[here, side:]
        norm = lax.rsqrt(jnp.maximum(s_re * s_re + s_im * s_im, 1.0))
        factor = 1.0 - amp_ref[k] * norm
        tall[:side, here] = s_re * factor
        tall[side:, here] = s_im * factor
    left = dot3(flipped, split(tall[...]))
    for k in range(count):
        here = slice(k * side, (k + 1) * side)
        wide[here, :side] = left[:side, here]
        wide[here, side:] = left[side:, here]
    wide[...] = dot3(split(wide[...]), table)

    term_re = jnp.zeros((side, side), F32)
    term_im = jnp.zeros((side, side), F32)
    weight = jnp.zeros((side, side), F32)
    for k in range(count):
        here = slice(k * side, (k + 1) * side)
        o_re = objects[k, 0]
        o_im = objects[k, 1]
        b_re = wide[here, :side]
        b_im = wide[here, side:]
        term_re = term_re + (o_re * b_re + o_im * b_im)
        term_im = term_im + (o_re * b_im - o_im * b_re)
        weight = weight + (o_re * o_re + o_im * o_im)
        where, row_shift, col_shift = place(k)
        pair = (probe_re * b_re + probe_im * b_im, probe_re * b_im - probe_im * b_re)
        for c in range(2):
            block = jnp.concatenate([pair[c], jnp.zeros((8, side), F32)], axis=0)
            block = pltpu.roll(block, row_shift, 0)
            block = jnp.concatenate([block, jnp.zeros((tall_side, side), F32)], axis=1)
            block = pltpu.roll(block, col_shift, 1)
            grad[(c,) + where] = grad[(c,) + where] + block
    term_ref[:, :side] = term_re
    term_ref[:, side : 2 * side] = term_im
    term_ref[:, 2 * side :] = weight
    up_ref[...] = grad[:, :half]
    down_ref[...] = grad[:, half + rows :]
    own_ref[...] = cur_ref[...] - STEP_SIZE * grad[:, half : half + rows]


def update_kernel(own_ref, above_ref, below_ref, dh_ref, dl_ref, updated_ref, send_ref, whole, sheet):
    half = above_ref.shape[1]
    rows = own_ref.shape[1]
    per = send_ref.shape[1] // 4
    whole[:, half : rows - half] = own_ref[:, half : rows - half]
    whole[:, :half] = own_ref[:, :half] - STEP_SIZE * above_ref[...]
    whole[:, rows - half :] = own_ref[:, rows - half :] - STEP_SIZE * below_ref[...]
    updated_ref[...] = whole[...]
    table = (dh_ref[...], dl_ref[...])
    for c in range(2):
        product = dot3(split(whole[c]), table)
        for part in range(per // 128):
            sheet[part] = product[:, part * 128 : (part + 1) * 128]
        for s in range(2):
            for part in range(per // 128):
                where = (2 * c + s) * per + part * 128
                send_ref[:, where : where + 128] = sheet[part, pl.ds(s, rows // 2, stride=2), :]


def volume_kernel(arrived_ref, ah_ref, al_ref, volume_ref, direction_ref):
    per = volume_ref.shape[-1]
    side = direction_ref.shape[-1]
    for c in range(2):
        where = 4 * per + c * side
        direction_ref[c] = arrived_ref[:, where : where + side]
    table = (ah_ref[...], al_ref[...])
    for c in range(2):
        for s in range(2):
            where = (2 * c + s) * per
            block = arrived_ref[:, where : where + per]
            volume_ref[c, s] = dot3(table, split(block))


def band(offset, weight, length):
    column = lax.broadcasted_iota(jnp.int32, (length, offset.shape[1]), 0)
    matrix = jnp.zeros(column.shape, F32)
    for step in range(weight.shape[0]):
        matrix = jnp.where(column == offset + step, weight[step : step + 1], matrix)
    return matrix


def band_kernel(do_ref, dw_ref, ao_ref, aw_ref, dh_ref, dl_ref, ah_ref, al_ref):
    dh_ref[...], dl_ref[...] = split(band(do_ref[...], dw_ref[...], dh_ref.shape[0]))
    turned = band(ao_ref[...], aw_ref[...], ah_ref.shape[1])
    ah_ref[...], al_ref[...] = split(turned.T)


def vmem(count):
    return [pl.BlockSpec(memory_space=pltpu.VMEM)] * count


def local(
    projection, probe, amplitude, pos_row, pos_col, ang_offset, ang_weight, det_offset, det_weight
):
    side = probe.shape[-1]
    half = side // 2
    rows = projection.shape[2]
    lanes = projection.shape[3]
    count = amplitude.shape[1]
    angles = lax.axis_size("angle")
    tiles = lax.axis_size("tile")
    radial = det_offset.shape[0]
    up = [(i, i + 1) for i in range(tiles - 1)]
    down = [(i + 1, i) for i in range(tiles - 1)]

    current = projection[:, 0]
    shape = jax.ShapeDtypeStruct
    before = lax.ppermute(current[:, rows - half :], "tile", up)
    after = lax.ppermute(current[:, :half], "tile", down)

    regular = ang_offset.shape[0]
    det_high, det_low, ang_high, ang_low = pl.pallas_call(
        band_kernel,
        out_shape=(shape((lanes, radial), BF16),) * 2 + (shape((regular, angles), BF16),) * 2,
        in_specs=vmem(4),
        out_specs=tuple(vmem(4)),
        name="bands",
    )(det_offset[None], det_weight.T, ang_offset[None], ang_weight.T)

    high, low = complex_table(side)
    own, upper, lower, terms = pl.pallas_call(
        patch_kernel,
        out_shape=(
            shape((2, rows, lanes), F32),
            shape((2, half, lanes), F32),
            shape((2, half, lanes), F32),
            shape((side, 3 * side), F32),
        ),
        in_specs=[pl.BlockSpec(memory_space=pltpu.SMEM)] * 2 + vmem(9),
        out_specs=tuple(vmem(4)),
        scratch_shapes=[
            pltpu.VMEM((2, rows + 2 * half, lanes), F32),
            pltpu.VMEM((2, rows + 2 * half, lanes), F32),
            pltpu.VMEM((count, 2, side, side), F32),
            pltpu.VMEM((2 * side, count * side), F32),
            pltpu.VMEM((count * side, 2 * side), F32),
        ],
        name="patches",
    )(
        pos_row, pos_col, current, before, after, probe, amplitude[0],
        jnp.asarray(high), jnp.asarray(low), jnp.asarray(high.T), jnp.asarray(low.T),
    )

    below = lax.ppermute(upper, "tile", down)
    above = lax.ppermute(lower, "tile", up)

    shares = lax.all_to_all(terms, "angle", 0, 0, tiled=True)

    updated, outgoing = pl.pallas_call(
        update_kernel,
        out_shape=(shape((2, rows, lanes), F32), shape((rows // 2, 4 * radial), F32)),
        in_specs=vmem(5),
        out_specs=tuple(vmem(2)),
        scratch_shapes=[
            pltpu.VMEM((2, rows, lanes), F32),
            pltpu.VMEM((radial // 128, rows, 128), F32),
        ],
        name="update",
    )(own, above, below, det_high, det_low)

    total = jnp.sum(shares, axis=0, keepdims=True)
    step = 1
    while step < tiles:
        pairs = [(i, i ^ step) for i in range(tiles)]
        total = total + lax.ppermute(total, "tile", pairs)
        step *= 2
    scale = lax.rsqrt(total[:, 2 * side :] + EPSILON)
    line = jnp.concatenate(
        [total[:, :side] * scale, total[:, side : 2 * side] * scale], axis=1
    )

    line = jnp.broadcast_to(line, (angles, 2 * side))
    arrived = lax.all_to_all(jnp.concatenate([outgoing, line], axis=1), "angle", 0, 0, tiled=True)

    volume, direction = pl.pallas_call(
        volume_kernel,
        out_shape=(shape((2, 2, regular, radial), F32), shape((2, side, side), F32)),
        in_specs=vmem(3),
        out_specs=tuple(vmem(2)),
        name="volume",
    )(arrived, ang_high, ang_low)
    return (updated[:, None], direction, volume[:, None])


def solution(mesh):
    in_specs = (
        P(None, "angle", "tile", None),
        P(),
        P("angle", "tile", None, None),
        P("angle", "tile"),
        P("angle", "tile"),
        P(),
        P(),
        P(),
        P(),
    )
    out_specs = (P(None, "angle", "tile", None), P(), P(None, "tile", "angle", None, None))
    return jax.shard_map(local, mesh=mesh, in_specs=in_specs, out_specs=out_specs, check_vma=False)
```

time: 594 us -> 125 us (0.21)
  the two profiles are of different devices: /device:TPU:1 before, /device:TPU:32 now
where the time goes in v1:
time: 125 us; the launch traced here: 124 us
  blocking collectives  47.4 us (38%)
  starting transfers between devices  38.8 us (31%)
  waiting for transfers between devices  17.5 us (14%)
  Pallas kernels  12.5 us (10%)
  local copies, waits for them, and re-layouts  6 us (5%)
  other arithmetic  1.29 us (1%)
    all_to_all x1, blocking collectives, local(): lax.all_to_all(jnp.concatenate([outgoing, line], axis=1), 'angle', 0, 0,...  47.4 us
    all_to_all x1, starting transfers between devices, local(): shares = lax.all_to_all(terms, 'angle', 0, 0, tiled=True)  21.8 us
    all_to_all x1, waiting for transfers between devices, local(): shares = lax.all_to_all(terms, 'angle', 0, 0, tiled=True)  15.6 us
    ppermute x2, starting transfers between devices, local(): total = total + lax.ppermute(total, 'tile', pairs)  6.82 us
    pallas_call x1, Pallas kernels, local(): pl.pallas_call(patch_kernel, out_shape=(shape((2, rows, lanes), F32), sha...  5.3 us
    ppermute x1, starting transfers between devices, local(): above = lax.ppermute(lower, 'tile', up)  4.61 us
    ppermute x1, starting transfers between devices, local(): before = lax.ppermute(current[:, rows - half:], 'tile', up)  3.05 us
    pallas_call x1, Pallas kernels, local(): pl.pallas_call(update_kernel, out_shape=(shape((2, rows, lanes), F32), sh...  2.98 us
  transfers between devices with their start and end apart: 7, of which 3 were waited for; matrix products, arithmetic and copies ran while one was open for 0% of the time, Pallas kernels for 4%

profile of v1, /device:TPU:32, one launch (start us, length us, event | category | flops | bytes accessed | tf_op | source)
XLA Modules:
  0.0 124.4 jit_solution(15858217734446422331)
XLA Ops:
  0.6 1.1 fusion.1
  1.7 1.3 %collective-permute-start.1 = (f32[2,64,512]{2,1,0:T(8,128)S(1)}, f32[2,64,512]{2,1,0:T(8,128)S(1)}, u32[]{:S(2)}, u32[]{:S(2)}) collective-permute-start(f32[2,64,512]{2,1,0:T(8,128)S(1)} %get-tuple-element.33), channel_id=1, source_target_pairs={{1,0},{2,1},{3,2},{5,4},{6,5},{7,6},{9,8},{10,9},{11,10},{13,12},{... | collective-permute-start | bytes 786440 | tf_op jit(solution)/shard_map/ppermute | solution.py:205
  3.0 3.0 %collective-permute-start = (f32[2,64,512]{2,1,0:T(8,128)S(1)}, f32[2,64,512]{2,1,0:T(8,128)S(1)}, u32[]{:S(2)}, u32[]{:S(2)}) collective-permute-start(f32[2,64,512]{2,1,0:T(8,128)S(1)} %get-tuple-element.34), channel_id=1, source_target_pairs={{0,1},{1,2},{2,3},{4,5},{5,6},{6,7},{8,9},{9,10},{10,11},{12,13},{... | collective-permute-start | bytes 786440 | tf_op jit(solution)/shard_map/ppermute | solution.py:204
  6.1 0.0 collective-permute-done.1.after_ref
  6.1 0.0 copy-start
  6.1 1.1 collective-permute-done.before_ref
  7.2 0.0 copy-done
  7.2 0.7 copy-done.1
  7.9 5.3 %patches.1 = (f32[2,256,512]{2,1,0:T(8,128)}, f32[2,64,512]{2,1,0:T(8,128)}, f32[2,64,512]{2,1,0:T(8,128)}, f32[128,384]{1,0:T(8,128)}) custom-call(s32[1,4]{1,0:T(1,128)} %row_ref.1, s32[1,4]{1,0:T(1,128)} %col_ref.1, f32[2,256,512]{2,1,0:T(8,128)} %bitcast.21, f32[2,64,512]{2,1,0:T(8,128)} %copy-done.1, f32[2,64,512]{2,1,0:T(8,128)} %copy-done, ...), custom_call_target="tpu_custom_call" | custom-call | tf_op jit(solution)/shard_map/patches/pallas_call | solution.py:217
  13.2 1.8 %copy.18 = f32[128,1,384]{2,1,0:T(1,128)} copy(f32[128,1,384]{2,0,1:T(8,128)} %bitcast.23) | data formatting | bytes 393216 | tf_op jit(solution)/shard_map/all_to_all | solution.py:243
  15.0 21.8 %all-to-all-start = ((f32[128,1,384]{2,1,0:T(1,128)}), f32[128,1,384]{2,1,0:T(1,128)S(1)}, u32[]{:S(2)}, u32[]{:S(2)}) async-start(f32[128,1,384]{2,1,0:T(1,128)} %copy.18), calls=%async_computation | async-start | bytes 393216 | tf_op jit(solution)/shard_map/all_to_all | solution.py:243
  36.8 0.0 copy-done.5
  36.8 4.6 %collective-permute-start.2 = (f32[2,64,512]{2,1,0:T(8,128)S(1)}, f32[2,64,512]{2,1,0:T(8,128)S(1)}, u32[]{:S(2)}, u32[]{:S(2)}) collective-permute-start(f32[2,64,512]{2,1,0:T(8,128)S(1)} %copy-done.5), channel_id=1, source_target_pairs={{0,1},{1,2},{2,3},{4,5},{5,6},{6,7},{8,9},{9,10},{10,11},{12,13},{... | collective-permute-start | bytes 786440 | tf_op jit(solution)/shard_map/ppermute | solution.py:241
  41.4 0.0 copy-done.4
  41.5 1.3 %collective-permute-start.3 = (f32[2,64,512]{2,1,0:T(8,128)S(1)}, f32[2,64,512]{2,1,0:T(8,128)S(1)}, u32[]{:S(2)}, u32[]{:S(2)}) collective-permute-start(f32[2,64,512]{2,1,0:T(8,128)S(1)} %copy-done.4), channel_id=1, source_target_pairs={{1,0},{2,1},{3,2},{5,4},{6,5},{7,6},{9,8},{10,9},{11,10},{13,12},{... | collective-permute-start | bytes 786440 | tf_op jit(solution)/shard_map/ppermute | solution.py:240
  42.8 15.6 %all-to-all-done = f32[128,1,384]{2,1,0:T(1,128)S(1)} async-done(((f32[128,1,384]{2,1,0:T(1,128)}), f32[128,1,384]{2,1,0:T(1,128)S(1)}, u32[]{:S(2)}, u32[]{:S(2)}) %all-to-all-start) | async-done | bytes 196640 | tf_op jit(solution)/shard_map/all_to_all | solution.py:243
  58.3 0.2 reduce_sum.9
  58.5 3.6 %collective-permute-start.4 = (f32[1,384]{1,0:T(1,128)S(1)}, f32[1,384]{1,0:T(1,128)S(1)}, u32[]{:S(2)}, u32[]{:S(2)}) collective-permute-start(f32[1,384]{1,0:T(1,128)S(1)} %broadcast_in_dim.25), channel_id=1, source_target_pairs={{0,1},{1,0},{2,3},{3,2},{4,5},{5,4},{6,7},{7,6},{8,9},{9,8},{10,11... | collective-permute-start | bytes 4616 | tf_op jit(solution)/shard_map/ppermute | solution.py:261
  62.2 0.8 collective-permute-done.4
  63.0 3.2 %collective-permute-start.5 = (f32[1,384]{1,0:T(1,128)S(1)}, f32[1,384]{1,0:T(1,128)S(1)}, u32[]{:S(2)}, u32[]{:S(2)}) collective-permute-start(f32[1,384]{1,0:T(1,128)S(1)} %reshape_add_fusion), channel_id=1, source_target_pairs={{0,2},{1,3},{2,0},{3,1},{4,6},{5,7},{6,4},{7,5},{8,10},{9,11},{10,... | collective-permute-start | bytes 4616 | tf_op jit(solution)/shard_map/ppermute | solution.py:261
  66.1 2.0 %bands.1 = (bf16[512,256]{1,0:T(8,128)(2,1)}, bf16[512,256]{1,0:T(8,128)(2,1)}, bf16[128,128]{1,0:T(8,128)(2,1)}, bf16[128,128]{1,0:T(8,128)(2,1)}) custom-call(s32[1,256]{1,0:T(1,128)} %bitcast.27, f32[4,256]{1,0:T(4,128)} %bitcast.25, s32[1,128]{1,0:T(1,128)} %bitcast.28, f32[4,128]{1,0:T(4,128)} %bitcast.26), custom_call_target="tpu_custom_call" | custom-call | tf_op jit(solution)/shard_map/bands/pallas_call | solution.py:208
  68.2 0.0 collective-permute-done.2.above_ref
  68.2 0.0 collective-permute-done.3.below_ref
  68.2 0.7 copy-done.2
  68.9 0.1 copy-done.3
  69.0 3.0 %update.1 = (f32[2,256,512]{2,1,0:T(8,128)}, f32[128,1024]{1,0:T(8,128)}) custom-call(f32[2,256,512]{2,1,0:T(8,128)} %get-tuple-element.15.own_ref, f32[2,64,512]{2,1,0:T(8,128)} %copy-done.2, f32[2,64,512]{2,1,0:T(8,128)} %copy-done.3, bf16[512,256]{1,0:T(8,128)(2,1)} %get-tuple-element.18.dh_ref, bf16[512,256]{1,0:T(8,128)(2,1)} %get-tuple-element.19.dl_ref), custom_call_target="tpu_custom_call" | custom-call | tf_op jit(solution)/shard_map/update/pallas_call | solution.py:245
  72.0 0.0 collective-permute-done.5
  72.0 1.1 maximum_bitcast_fusion
  73.1 0.7 copy.19
  73.8 47.4 %all_to_all.20 = f32[128,1,1280]{2,1,0:T(1,128)S(1)} all-to-all(f32[128,1,1280]{2,1,0:T(1,128)S(1)} %copy.19), channel_id=1, replica_groups=mesh['angle'=128,'tile'=4] {'angle'}, dimensions={0} | all-to-all | bytes 1310720 | tf_op jit(solution)/shard_map/all_to_all | solution.py:269
  121.2 0.9 copy.24
  122.1 2.3 %volume.1 = (f32[2,2,128,256]{3,2,1,0:T(8,128)}, f32[2,128,128]{2,1,0:T(8,128)}) custom-call(f32[128,1280]{1,0:T(8,128)} %bitcast.19, bf16[128,128]{1,0:T(8,128)(2,1)} %get-tuple-element.23.ah_ref, bf16[128,128]{1,0:T(8,128)(2,1)} %get-tuple-element.24.al_ref), custom_call_target="tpu_custom_call" | custom-call | tf_op jit(solution)/shard_map/volume/pallas_call | solution.py:271
  (11 shorter events, 0.0 us)
Async XLA Ops:
  1.7 4.4 %collective-permute-start.1 = (f32[2,64,512]{2,1,0:T(8,128)S(1)}, f32[2,64,512]{2,1,0:T(8,128)S(1)}, u32[]{:S(2)}, u32[]{:S(2)}) collective-permute-start(f32[2,64,512]{2,1,0:T(8,128)S(1)} %get-tuple-element.33), channel_id=1, source_target_pairs={{1,0},{2,1},{3,2},{5,4},{6,5},{7,6},{9,8},{10,9},{11,10},{13,12},{... | collective-permute-start | bytes 786440 | tf_op jit(solution)/shard_map/ppermute | solution.py:205
  3.0 4.2 %collective-permute-start = (f32[2,64,512]{2,1,0:T(8,128)S(1)}, f32[2,64,512]{2,1,0:T(8,128)S(1)}, u32[]{:S(2)}, u32[]{:S(2)}) collective-permute-start(f32[2,64,512]{2,1,0:T(8,128)S(1)} %get-tuple-element.34), channel_id=1, source_target_pairs={{0,1},{1,2},{2,3},{4,5},{5,6},{6,7},{8,9},{9,10},{10,11},{12,13},{... | collective-permute-start | bytes 786440 | tf_op jit(solution)/shard_map/ppermute | solution.py:204
  6.1 1.1 copy-start
  7.2 0.7 copy-start.1
  13.2 23.6 %copy-start.5 = (f32[2,64,512]{2,1,0:T(8,128)S(1)}, f32[2,64,512]{2,1,0:T(8,128)}, u32[]{:S(2)}) copy-start(f32[2,64,512]{2,1,0:T(8,128)} %get-tuple-element.16) | copy-start | bytes 786436
  15.0 26.4 %copy-start.4 = (f32[2,64,512]{2,1,0:T(8,128)S(1)}, f32[2,64,512]{2,1,0:T(8,128)}, u32[]{:S(2)}) copy-start(f32[2,64,512]{2,1,0:T(8,128)} %get-tuple-element.17) | copy-start | bytes 786436
  15.0 43.3 %all-to-all-start = ((f32[128,1,384]{2,1,0:T(1,128)}), f32[128,1,384]{2,1,0:T(1,128)S(1)}, u32[]{:S(2)}, u32[]{:S(2)}) async-start(f32[128,1,384]{2,1,0:T(1,128)} %copy.18), calls=%async_computation | async-start | bytes 393216 | tf_op jit(solution)/shard_map/all_to_all | solution.py:243
  36.8 31.3 %collective-permute-start.2 = (f32[2,64,512]{2,1,0:T(8,128)S(1)}, f32[2,64,512]{2,1,0:T(8,128)S(1)}, u32[]{:S(2)}, u32[]{:S(2)}) collective-permute-start(f32[2,64,512]{2,1,0:T(8,128)S(1)} %copy-done.5), channel_id=1, source_target_pairs={{0,1},{1,2},{2,3},{4,5},{5,6},{6,7},{8,9},{9,10},{10,11},{12,13},{... | collective-permute-start | bytes 786440 | tf_op jit(solution)/shard_map/ppermute | solution.py:241
  41.5 26.7 %collective-permute-start.3 = (f32[2,64,512]{2,1,0:T(8,128)S(1)}, f32[2,64,512]{2,1,0:T(8,128)S(1)}, u32[]{:S(2)}, u32[]{:S(2)}) collective-permute-start(f32[2,64,512]{2,1,0:T(8,128)S(1)} %copy-done.4), channel_id=1, source_target_pairs={{1,0},{2,1},{3,2},{5,4},{6,5},{7,6},{9,8},{10,9},{11,10},{13,12},{... | collective-permute-start | bytes 786440 | tf_op jit(solution)/shard_map/ppermute | solution.py:240
  58.5 4.4 %collective-permute-start.4 = (f32[1,384]{1,0:T(1,128)S(1)}, f32[1,384]{1,0:T(1,128)S(1)}, u32[]{:S(2)}, u32[]{:S(2)}) collective-permute-start(f32[1,384]{1,0:T(1,128)S(1)} %broadcast_in_dim.25), channel_id=1, source_target_pairs={{0,1},{1,0},{2,3},{3,2},{4,5},{5,4},{6,7},{7,6},{8,9},{9,8},{10,11... | collective-permute-start | bytes 4616 | tf_op jit(solution)/shard_map/ppermute | solution.py:261
  63.0 9.0 %collective-permute-start.5 = (f32[1,384]{1,0:T(1,128)S(1)}, f32[1,384]{1,0:T(1,128)S(1)}, u32[]{:S(2)}, u32[]{:S(2)}) collective-permute-start(f32[1,384]{1,0:T(1,128)S(1)} %reshape_add_fusion), channel_id=1, source_target_pairs={{0,2},{1,3},{2,0},{3,1},{4,6},{5,7},{6,4},{7,5},{8,10},{9,11},{10,... | collective-permute-start | bytes 4616 | tf_op jit(solution)/shard_map/ppermute | solution.py:261
  68.2 0.7 copy-start.2
  68.2 0.8 copy-start.3

commit v2 on v1

--- a/solution.py
+++ b/solution.py
@@ -126,9 +126,14 @@
             block = jnp.concatenate([block, jnp.zeros((tall_side, side), F32)], axis=1)
             block = pltpu.roll(block, col_shift, 1)
             grad[(c,) + where] = grad[(c,) + where] + block
-    term_ref[:, :side] = term_re
-    term_ref[:, side : 2 * side] = term_im
-    term_ref[:, 2 * side :] = weight
+    tiles = term_ref.shape[0] // side
+    part = side // tiles
+    lane = lax.broadcasted_iota(jnp.int32, (side, side), 1)
+    for t in range(tiles):
+        share = pltpu.roll(weight, (2 * part - part * t) % side, 1)
+        share = jnp.where(lane < 2 * part, pltpu.roll(term_im, (part - part * t) % side, 1), share)
+        share = jnp.where(lane < part, pltpu.roll(term_re, -part * t % side, 1), share)
+        term_ref[pl.ds(t, side, stride=tiles), :] = share
     up_ref[...] = grad[:, :half]
     down_ref[...] = grad[:, half + rows :]
     own_ref[...] = cur_ref[...] - STEP_SIZE * grad[:, half : half + rows]
@@ -137,7 +142,8 @@
 def update_kernel(own_ref, above_ref, below_ref, dh_ref, dl_ref, updated_ref, send_ref, whole, sheet):
     half = above_ref.shape[1]
     rows = own_ref.shape[1]
-    per = send_ref.shape[1] // 4
+    per = dh_ref.shape[1]
+    pieces = send_ref.shape[0] // (rows // 2)
     whole[:, half : rows - half] = own_ref[:, half : rows - half]
     whole[:, :half] = own_ref[:, :half] - STEP_SIZE * above_ref[...]
     whole[:, rows - half :] = own_ref[:, rows - half :] - STEP_SIZE * below_ref[...]
@@ -149,22 +155,56 @@
             sheet[part] = product[:, part * 128 : (part + 1) * 128]
         for s in range(2):
             for part in range(per // 128):
-                where = (2 * c + s) * per + part * 128
-                send_ref[:, where : where + 128] = sheet[part, pl.ds(s, rows // 2, stride=2), :]
-
-
-def volume_kernel(arrived_ref, ah_ref, al_ref, volume_ref, direction_ref):
-    per = volume_ref.shape[-1]
-    side = direction_ref.shape[-1]
-    for c in range(2):
-        where = 4 * per + c * side
-        direction_ref[c] = arrived_ref[:, where : where + side]
+                piece = (2 * c + s) * (per // 128) + part
+                rows_of = pl.ds(piece, rows // 2, stride=pieces)
+                send_ref[rows_of, :] = sheet[part, pl.ds(s, rows // 2, stride=2), :]
+
+
+def line_kernel(share_ref, packed_ref, sent_ref):
+    lanes = share_ref.shape[1]
+    part = lanes // 4
+    total = jnp.sum(share_ref[...], axis=0, keepdims=True)
+    total = jnp.broadcast_to(total, (8, lanes))
+    lane = lax.broadcasted_iota(jnp.int32, (8, lanes), 1)
+    weight = jnp.where(
+        lane < part, pltpu.roll(total, lanes - 2 * part, 1), pltpu.roll(total, lanes - part, 1)
+    )
+    line = jnp.where(lane < 2 * part, total * lax.rsqrt(weight + EPSILON), 0.0)
+    peers = lanes
+    pieces = sent_ref.shape[0] // peers
+    sent_ref[...] = packed_ref[...]
+    sent_ref[pl.ds(pieces - 1, peers, stride=pieces), :] = jnp.broadcast_to(line[:1], (peers, lanes))
+
+
+def volume_kernel(arrived_ref, ah_ref, al_ref, volume_ref):
+    parts = volume_ref.shape[-1] // 128
+    angles = ah_ref.shape[1]
+    pieces = arrived_ref.shape[0] // angles
     table = (ah_ref[...], al_ref[...])
     for c in range(2):
         for s in range(2):
-            where = (2 * c + s) * per
-            block = arrived_ref[:, where : where + per]
-            volume_ref[c, s] = dot3(table, split(block))
+            blocks = [
+                arrived_ref[pl.ds((2 * c + s) * parts + part, angles, stride=pieces), :]
+                for part in range(parts)
+            ]
+            volume_ref[c, s] = dot3(table, split(jnp.concatenate(blocks, axis=1)))
+
+
+def direction_kernel(me_ref, *refs):
+    direction_ref = refs[-1]
+    side = direction_ref.shape[-1]
+    tiles = len(refs) - 1
+    part = side // tiles
+    lane = lax.broadcasted_iota(jnp.int32, (side, side), 1)
+    whole = [jnp.zeros((side, side), F32)] * 2
+    for k in range(tiles):
+        source = lax.rem(me_ref[0] + tiles - k, tiles)
+        here = (lane >= source * part) & (lane < (source + 1) * part)
+        for c in range(2):
+            shift = lax.rem(source * part + side - c * part, side)
+            whole[c] = jnp.where(here, pltpu.roll(refs[k][...], shift, 1), whole[c])
+    for c in range(2):
+        direction_ref[c] = whole[c]
 
 
 def band(offset, weight, length):
@@ -179,6 +219,10 @@
     dh_ref[...], dl_ref[...] = split(band(do_ref[...], dw_ref[...], dh_ref.shape[0]))
     turned = band(ao_ref[...], aw_ref[...], ah_ref.shape[1])
     ah_ref[...], al_ref[...] = split(turned.T)
+
+
+def held(value):
+    return pltpu.with_memory_space_constraint(value, pltpu.VMEM)
 
 
 def vmem(count):
@@ -207,7 +251,8 @@
     regular = ang_offset.shape[0]
     det_high, det_low, ang_high, ang_low = pl.pallas_call(
         band_kernel,
-        out_shape=(shape((lanes, radial), BF16),) * 2 + (shape((regular, angles), BF16),) * 2,
+        out_shape=(pltpu.VMEM((lanes, radial), BF16),) * 2
+        + (pltpu.VMEM((regular, angles), BF16),) * 2,
         in_specs=vmem(4),
         out_specs=tuple(vmem(4)),
         name="bands",
@@ -218,9 +263,9 @@
         patch_kernel,
         out_shape=(
             shape((2, rows, lanes), F32),
-            shape((2, half, lanes), F32),
-            shape((2, half, lanes), F32),
-            shape((side, 3 * side), F32),
+            pltpu.VMEM((2, half, lanes), F32),
+            pltpu.VMEM((2, half, lanes), F32),
+            pltpu.VMEM((side * tiles, side), F32),
         ),
         in_specs=[pl.BlockSpec(memory_space=pltpu.SMEM)] * 2 + vmem(9),
         out_specs=tuple(vmem(4)),
@@ -233,18 +278,20 @@
         ],
         name="patches",
     )(
-        pos_row, pos_col, current, before, after, probe, amplitude[0],
+        pos_row, pos_col, current, held(before), held(after), probe, amplitude[0],
         jnp.asarray(high), jnp.asarray(low), jnp.asarray(high.T), jnp.asarray(low.T),
     )
+
+    shares = lax.all_to_all(terms, ("angle", "tile"), 0, 0, tiled=True)
 
     below = lax.ppermute(upper, "tile", down)
     above = lax.ppermute(lower, "tile", up)
 
-    shares = lax.all_to_all(terms, "angle", 0, 0, tiled=True)
-
-    updated, outgoing = pl.pallas_call(
+    peers = rows // 2
+    pieces = 4 * radial // 128 + 1
+    updated, packed = pl.pallas_call(
         update_kernel,
-        out_shape=(shape((2, rows, lanes), F32), shape((rows // 2, 4 * radial), F32)),
+        out_shape=(shape((2, rows, lanes), F32), pltpu.VMEM((peers * pieces, 128), F32)),
         in_specs=vmem(5),
         out_specs=tuple(vmem(2)),
         scratch_shapes=[
@@ -252,29 +299,42 @@
             pltpu.VMEM((radial // 128, rows, 128), F32),
         ],
         name="update",
-    )(own, above, below, det_high, det_low)
-
-    total = jnp.sum(shares, axis=0, keepdims=True)
-    step = 1
-    while step < tiles:
-        pairs = [(i, i ^ step) for i in range(tiles)]
-        total = total + lax.ppermute(total, "tile", pairs)
-        step *= 2
-    scale = lax.rsqrt(total[:, 2 * side :] + EPSILON)
-    line = jnp.concatenate(
-        [total[:, :side] * scale, total[:, side : 2 * side] * scale], axis=1
-    )
-
-    line = jnp.broadcast_to(line, (angles, 2 * side))
-    arrived = lax.all_to_all(jnp.concatenate([outgoing, line], axis=1), "angle", 0, 0, tiled=True)
-
-    volume, direction = pl.pallas_call(
+    )(own, held(above), held(below), held(det_high), held(det_low))
+
+    sent = pl.pallas_call(
+        line_kernel,
+        out_shape=pltpu.VMEM((peers * pieces, 128), F32),
+        in_specs=vmem(2),
+        out_specs=vmem(1)[0],
+        name="line",
+    )(held(shares), held(packed))
+
+    arrived = lax.all_to_all(
+        sent.reshape(peers, pieces * 128), "angle", 0, 0, tiled=True
+    )
+
+    mine = lax.slice(
+        arrived.reshape(peers * pieces, 128),
+        (pieces - 1, 0), (peers * pieces, 128), (pieces, 1),
+    )
+    quarters = [mine] + [
+        lax.ppermute(mine, "tile", [(i, (i + k) % tiles) for i in range(tiles)])
+        for k in range(1, tiles)
+    ]
+    volume = pl.pallas_call(
         volume_kernel,
-        out_shape=(shape((2, 2, regular, radial), F32), shape((2, side, side), F32)),
+        out_shape=shape((2, 2, regular, radial), F32),
         in_specs=vmem(3),
-        out_specs=tuple(vmem(2)),
+        out_specs=vmem(1)[0],
         name="volume",
-    )(arrived, ang_high, ang_low)
+    )(held(arrived.reshape(peers * pieces, 128)), held(ang_high), held(ang_low))
+    direction = pl.pallas_call(
+        direction_kernel,
+        out_shape=shape((2, side, side), F32),
+        in_specs=[pl.BlockSpec(memory_space=pltpu.SMEM)] + vmem(tiles),
+        out_specs=vmem(1)[0],
+        name="direction",
+    )(lax.axis_index("tile")[None], *map(held, quarters))
     return (updated[:, None], direction, volume[:, None])
 
 

time: 125 us -> 123 us (0.984)
  the two profiles are of different devices: /device:TPU:32 before, /device:TPU:1 now
where the time goes in v2:
time: 123 us
  starting transfers between devices  46.4 us (38%)
  blocking collectives  45.4 us (37%)
  waiting for transfers between devices  18 us (15%)
  Pallas kernels  11.2 us (9%)
    all_to_all x1, blocking collectives, local(): lax.all_to_all(sent.reshape(peers, pieces * 128), 'angle', 0, 0, tiled=True)  45.4 us
    all_to_all x1, starting transfers between devices, local(): shares = lax.all_to_all(terms, ('angle', 'tile'), 0, 0, tiled=True)  22.6 us
    all_to_all x1, waiting for transfers between devices, local(): shares = lax.all_to_all(terms, ('angle', 'tile'), 0, 0, tiled=True)  9.96 us
    ppermute x3, starting transfers between devices, local(): lax.ppermute(mine, 'tile', [(i, (i + k) % tiles) for i in range(tiles)])  6.25 us
    ppermute x1, starting transfers between devices, local(): after = lax.ppermute(current[:, :half], 'tile', down)  5.55 us
    pallas_call x1, Pallas kernels, local(): pl.pallas_call(patch_kernel, out_shape=(shape((2, rows, lanes), F32), plt...  5.32 us
    ppermute x1, starting transfers between devices, local(): before = lax.ppermute(current[:, rows - half:], 'tile', up)  4.5 us
    ppermute x1, starting transfers between devices, local(): below = lax.ppermute(upper, 'tile', down)  3.98 us
  transfers between devices with their start and end apart: 8, of which 4 were waited for; matrix products, arithmetic and copies ran while one was open for 0% of the time, Pallas kernels for 4%

profile of v2, /device:TPU:1, one launch (start us, length us, event | category | flops | bytes accessed | tf_op | source)
XLA Modules:
  0.0 122.8 jit_solution(13929673873571420442)
XLA Ops:
  0.6 1.1 fusion
  1.7 4.5 %collective-permute-start = (f32[2,64,512]{2,1,0:T(8,128)S(1)}, f32[2,64,512]{2,1,0:T(8,128)S(1)}, u32[]{:S(2)}, u32[]{:S(2)}) collective-permute-start(f32[2,64,512]{2,1,0:T(8,128)S(1)} %get-tuple-element.30), channel_id=1, source_target_pairs={{0,1},{1,2},{2,3},{4,5},{5,6},{6,7},{8,9},{9,10},{10,11},{12,13},{... | collective-permute-start | bytes 786440 | tf_op jit(solution)/shard_map/ppermute | solution.py:248
  6.2 5.6 %collective-permute-start.1 = (f32[2,64,512]{2,1,0:T(8,128)S(1)}, f32[2,64,512]{2,1,0:T(8,128)S(1)}, u32[]{:S(2)}, u32[]{:S(2)}) collective-permute-start(f32[2,64,512]{2,1,0:T(8,128)S(1)} %get-tuple-element.29), channel_id=1, source_target_pairs={{1,0},{2,1},{3,2},{5,4},{6,5},{7,6},{9,8},{10,9},{11,10},{13,12},{... | collective-permute-start | bytes 786440 | tf_op jit(solution)/shard_map/ppermute | solution.py:249
  11.8 0.0 collective-permute-done.before_ref
  11.8 2.1 %collective-permute-done.1.after_ref = f32[2,64,512]{2,1,0:T(8,128)S(1)} collective-permute-done((f32[2,64,512]{2,1,0:T(8,128)S(1)}, f32[2,64,512]{2,1,0:T(8,128)S(1)}, u32[]{:S(2)}, u32[]{:S(2)}) %collective-permute-start.1) | collective-permute-done | bytes 262176 | tf_op jit(solution)/shard_map/ppermute | solution.py:249
  13.9 5.3 %patches.1 = (f32[2,256,512]{2,1,0:T(8,128)}, f32[2,64,512]{2,1,0:T(8,128)S(1)}, f32[2,64,512]{2,1,0:T(8,128)S(1)}, f32[512,128]{1,0:T(8,128)}) custom-call(s32[1,4]{1,0:T(1,128)} %row_ref.1, s32[1,4]{1,0:T(1,128)} %col_ref.1, f32[2,256,512]{2,1,0:T(8,128)} %bitcast.24, f32[2,64,512]{2,1,0:T(8,128)S(1)} %collective-permute-done.before_ref, ...), custom_call_target="tpu_custom_call" | custom-call | tf_op jit(solution)/shard_map/patches/pallas_call | solution.py:262
  19.2 22.6 %all-to-all-start = ((f32[512,1,128]{2,1,0:T(1,128)}), f32[512,1,128]{2,1,0:T(1,128)S(1)}, u32[]{:S(2)}, u32[]{:S(2)}) async-start(f32[512,1,128]{2,1,0:T(1,128)} %bitcast.10), calls=%async_computation | async-start | bytes 524288 | tf_op jit(solution)/shard_map/all_to_all | solution.py:285
  41.9 3.5 %collective-permute-start.2 = (f32[2,64,512]{2,1,0:T(8,128)S(1)}, f32[2,64,512]{2,1,0:T(8,128)S(1)}, u32[]{:S(2)}, u32[]{:S(2)}) collective-permute-start(f32[2,64,512]{2,1,0:T(8,128)S(1)} %get-tuple-element.14), channel_id=1, source_target_pairs={{0,1},{1,2},{2,3},{4,5},{5,6},{6,7},{8,9},{9,10},{10,11},{12,13},{... | collective-permute-start | bytes 786440 | tf_op jit(solution)/shard_map/ppermute | solution.py:288
  45.4 4.0 %collective-permute-start.3 = (f32[2,64,512]{2,1,0:T(8,128)S(1)}, f32[2,64,512]{2,1,0:T(8,128)S(1)}, u32[]{:S(2)}, u32[]{:S(2)}) collective-permute-start(f32[2,64,512]{2,1,0:T(8,128)S(1)} %get-tuple-element.15), channel_id=1, source_target_pairs={{1,0},{2,1},{3,2},{5,4},{6,5},{7,6},{9,8},{10,9},{11,10},{13,12},{... | collective-permute-start | bytes 786440 | tf_op jit(solution)/shard_map/ppermute | solution.py:287
  49.4 1.3 %bands.1 = (bf16[512,256]{1,0:T(8,128)(2,1)S(1)}, bf16[512,256]{1,0:T(8,128)(2,1)S(1)}, bf16[128,128]{1,0:T(8,128)(2,1)S(1)}, bf16[128,128]{1,0:T(8,128)(2,1)S(1)}) custom-call(s32[1,256]{1,0:T(1,128)} %bitcast.29, f32[4,256]{1,0:T(4,128)} %bitcast.27, s32[1,128]{1,0:T(1,128)} %bitcast.30, f32[4,128]{1,0:T(4,128)} %bitcast.28), custom_call_target="tpu_custom_call" | custom-call | tf_op jit(solution)/shard_map/bands/pallas_call | solution.py:252
  50.6 0.0 collective-permute-done.2.above_ref
  50.7 3.5 %collective-permute-done.3.below_ref = f32[2,64,512]{2,1,0:T(8,128)S(1)} collective-permute-done((f32[2,64,512]{2,1,0:T(8,128)S(1)}, f32[2,64,512]{2,1,0:T(8,128)S(1)}, u32[]{:S(2)}, u32[]{:S(2)}) %collective-permute-start.3) | collective-permute-done | bytes 262176 | tf_op jit(solution)/shard_map/ppermute | solution.py:287
  54.1 2.4 %update.1 = (f32[2,256,512]{2,1,0:T(8,128)}, f32[1152,128]{1,0:T(8,128)S(1)}) custom-call(f32[2,256,512]{2,1,0:T(8,128)} %get-tuple-element.13.own_ref, f32[2,64,512]{2,1,0:T(8,128)S(1)} %collective-permute-done.2.above_ref, f32[2,64,512]{2,1,0:T(8,128)S(1)} %collective-permute-done.3.below_ref, bf16[512,256]{1,0:T(8,128)(2,1)S(1)} %get-tuple-element.16.dh_ref, ...), custom_call_target="tpu_custom_call" | custom-call | tf_op jit(solution)/shard_map/update/pallas_call | solution.py:292
  56.6 10.0 %all-to-all-done = f32[512,1,128]{2,1,0:T(1,128)S(1)} async-done(((f32[512,1,128]{2,1,0:T(1,128)}), f32[512,1,128]{2,1,0:T(1,128)S(1)}, u32[]{:S(2)}, u32[]{:S(2)}) %all-to-all-start) | async-done | bytes 262176 | tf_op jit(solution)/shard_map/all_to_all | solution.py:285
  66.5 0.2 line.1
  66.7 45.4 %all_to_all.20 = f32[128,1,1152]{2,1,0:T(1,128)S(1)} all-to-all(f32[128,1,1152]{2,1,0:T(1,128)S(1)} %bitcast.21), channel_id=1, replica_groups=mesh['angle'=128,'tile'=4] {'angle'}, dimensions={0} | all-to-all | bytes 1179648 | tf_op jit(solution)/shard_map/all_to_all | solution.py:312
  112.1 1.9 %collective-permute-start.4 = (f32[128,128]{1,0:T(8,128)S(1)}, f32[128,128]{1,0:T(8,128)S(1)}, u32[]{:S(2)}, u32[]{:S(2)}) collective-permute-start(f32[128,128]{1,0:T(8,128)S(1)} %slice.11.refs_0_), channel_id=1, source_target_pairs={{0,1},{1,2},{2,3},{3,0},{4,5},{5,6},{6,7},{7,4},{8,9},{9,10},{10,1... | collective-permute-start | bytes 196616 | tf_op jit(solution)/shard_map/ppermute | solution.py:321
  114.1 1.9 %collective-permute-start.5 = (f32[128,128]{1,0:T(8,128)S(1)}, f32[128,128]{1,0:T(8,128)S(1)}, u32[]{:S(2)}, u32[]{:S(2)}) collective-permute-start(f32[128,128]{1,0:T(8,128)S(1)} %slice.11.refs_0_), channel_id=1, source_target_pairs={{0,2},{1,3},{2,0},{3,1},{4,6},{5,7},{6,4},{7,5},{8,10},{9,11},{10,... | collective-permute-start | bytes 196616 | tf_op jit(solution)/shard_map/ppermute | solution.py:321
  116.0 2.4 %collective-permute-start.6 = (f32[128,128]{1,0:T(8,128)S(1)}, f32[128,128]{1,0:T(8,128)S(1)}, u32[]{:S(2)}, u32[]{:S(2)}) collective-permute-start(f32[128,128]{1,0:T(8,128)S(1)} %slice.11.refs_0_), channel_id=1, source_target_pairs={{0,3},{1,0},{2,1},{3,2},{4,7},{5,4},{6,5},{7,6},{8,11},{9,8},{10,9... | collective-permute-start | bytes 196616 | tf_op jit(solution)/shard_map/ppermute | solution.py:321
  118.4 1.1 volume.1
  119.6 0.0 collective-permute-done.4.refs_1_
  119.6 0.0 collective-permute-done.5.refs_2_
  119.6 2.4 %collective-permute-done.6.refs_3_ = f32[128,128]{1,0:T(8,128)S(1)} collective-permute-done((f32[128,128]{1,0:T(8,128)S(1)}, f32[128,128]{1,0:T(8,128)S(1)}, u32[]{:S(2)}, u32[]{:S(2)}) %collective-permute-start.6) | collective-permute-done | bytes 65568 | tf_op jit(solution)/shard_map/ppermute | solution.py:321
  122.0 0.9 direction.1
  (1 shorter events, 0.0 us)
Async XLA Ops:
  1.7 10.1 %collective-permute-start = (f32[2,64,512]{2,1,0:T(8,128)S(1)}, f32[2,64,512]{2,1,0:T(8,128)S(1)}, u32[]{:S(2)}, u32[]{:S(2)}) collective-permute-start(f32[2,64,512]{2,1,0:T(8,128)S(1)} %get-tuple-element.30), channel_id=1, source_target_pairs={{0,1},{1,2},{2,3},{4,5},{5,6},{6,7},{8,9},{9,10},{10,11},{12,13},{... | collective-permute-start | bytes 786440 | tf_op jit(solution)/shard_map/ppermute | solution.py:248
  6.2 7.7 %collective-permute-start.1 = (f32[2,64,512]{2,1,0:T(8,128)S(1)}, f32[2,64,512]{2,1,0:T(8,128)S(1)}, u32[]{:S(2)}, u32[]{:S(2)}) collective-permute-start(f32[2,64,512]{2,1,0:T(8,128)S(1)} %get-tuple-element.29), channel_id=1, source_target_pairs={{1,0},{2,1},{3,2},{5,4},{6,5},{7,6},{9,8},{10,9},{11,10},{13,12},{... | collective-permute-start | bytes 786440 | tf_op jit(solution)/shard_map/ppermute | solution.py:249
  19.2 47.3 %all-to-all-start = ((f32[512,1,128]{2,1,0:T(1,128)}), f32[512,1,128]{2,1,0:T(1,128)S(1)}, u32[]{:S(2)}, u32[]{:S(2)}) async-start(f32[512,1,128]{2,1,0:T(1,128)} %bitcast.10), calls=%async_computation | async-start | bytes 524288 | tf_op jit(solution)/shard_map/all_to_all | solution.py:285
  41.9 8.8 %collective-permute-start.2 = (f32[2,64,512]{2,1,0:T(8,128)S(1)}, f32[2,64,512]{2,1,0:T(8,128)S(1)}, u32[]{:S(2)}, u32[]{:S(2)}) collective-permute-start(f32[2,64,512]{2,1,0:T(8,128)S(1)} %get-tuple-element.14), channel_id=1, source_target_pairs={{0,1},{1,2},{2,3},{4,5},{5,6},{6,7},{8,9},{9,10},{10,11},{12,13},{... | collective-permute-start | bytes 786440 | tf_op jit(solution)/shard_map/ppermute | solution.py:288
  45.4 8.7 %collective-permute-start.3 = (f32[2,64,512]{2,1,0:T(8,128)S(1)}, f32[2,64,512]{2,1,0:T(8,128)S(1)}, u32[]{:S(2)}, u32[]{:S(2)}) collective-permute-start(f32[2,64,512]{2,1,0:T(8,128)S(1)} %get-tuple-element.15), channel_id=1, source_target_pairs={{1,0},{2,1},{3,2},{5,4},{6,5},{7,6},{9,8},{10,9},{11,10},{13,12},{... | collective-permute-start | bytes 786440 | tf_op jit(solution)/shard_map/ppermute | solution.py:287
  112.1 7.4 %collective-permute-start.4 = (f32[128,128]{1,0:T(8,128)S(1)}, f32[128,128]{1,0:T(8,128)S(1)}, u32[]{:S(2)}, u32[]{:S(2)}) collective-permute-start(f32[128,128]{1,0:T(8,128)S(1)} %slice.11.refs_0_), channel_id=1, source_target_pairs={{0,1},{1,2},{2,3},{3,0},{4,5},{5,6},{6,7},{7,4},{8,9},{9,10},{10,1... | collective-permute-start | bytes 196616 | tf_op jit(solution)/shard_map/ppermute | solution.py:321
  114.1 5.5 %collective-permute-start.5 = (f32[128,128]{1,0:T(8,128)S(1)}, f32[128,128]{1,0:T(8,128)S(1)}, u32[]{:S(2)}, u32[]{:S(2)}) collective-permute-start(f32[128,128]{1,0:T(8,128)S(1)} %slice.11.refs_0_), channel_id=1, source_target_pairs={{0,2},{1,3},{2,0},{3,1},{4,6},{5,7},{6,4},{7,5},{8,10},{9,11},{10,... | collective-permute-start | bytes 196616 | tf_op jit(solution)/shard_map/ppermute | solution.py:321
  116.0 6.0 %collective-permute-start.6 = (f32[128,128]{1,0:T(8,128)S(1)}, f32[128,128]{1,0:T(8,128)S(1)}, u32[]{:S(2)}, u32[]{:S(2)}) collective-permute-start(f32[128,128]{1,0:T(8,128)S(1)} %slice.11.refs_0_), channel_id=1, source_target_pairs={{0,3},{1,0},{2,1},{3,2},{4,7},{5,4},{6,5},{7,6},{8,11},{9,8},{10,9... | collective-permute-start | bytes 196616 | tf_op jit(solution)/shard_map/ppermute | solution.py:321

commit v3 on v1

v3 whole, which is shorter than its diff:
```python
import functools

import jax
import jax.numpy as jnp
import numpy as np
from jax import lax
from jax.experimental import pallas as pl
from jax.experimental.pallas import tpu as pltpu
from jax.sharding import PartitionSpec as P

STEP_SIZE = 0.1
EPSILON = 1e-06
F32 = jnp.float32
BF16 = jnp.bfloat16


def complex_table(length):
    counter = np.arange(length)
    angle = (counter[:, None] * counter[None, :] % length) * (2.0 * np.pi / length)
    re = np.cos(angle) / np.sqrt(length)
    im = -np.sin(angle) / np.sqrt(length)
    table = np.block([[re, -im], [im, re]]).astype(np.float32)
    high = table.astype(BF16)
    low = (table - high.astype(np.float32)).astype(BF16)
    return high, low


def split(value):
    high = value.astype(BF16)
    low = (value - high.astype(F32)).astype(BF16)
    return high, low


def dot3(left, right):
    mul = functools.partial(jnp.dot, preferred_element_type=F32)
    return mul(left[0], right[0]) + (mul(left[0], right[1]) + mul(left[1], right[0]))


def places(row_ref, col_ref, k, side, lanes):
    row = row_ref[0, k]
    col = col_ref[0, k]
    first = lax.div(row, 8)
    base = jnp.minimum(lax.div(col, side), lanes // side - 2)
    where = (
        pl.ds(pl.multiple_of(first * 8, 8), side + 8),
        pl.ds(pl.multiple_of(base * side, side), 2 * side),
    )
    return where, row - first * 8, col - base * side


def terms_kernel(
    row_ref, col_ref, cur_ref, before_ref, after_ref, probe_in, amp_in, high_in, low_in,
    term_ref, back_ref,
    padded, objects, tall, wide, probe_ref, amp_ref, high_ref, low_ref, sems,
):
    side = probe_ref.shape[-1]
    half = side // 2
    rows = cur_ref.shape[1]
    lanes = cur_ref.shape[2]
    count = amp_ref.shape[0]
    loads = [
        pltpu.make_async_copy(source, target, sems.at[i])
        for i, (source, target) in enumerate(
            ((probe_in, probe_ref), (high_in, high_ref), (low_in, low_ref), (amp_in, amp_ref))
        )
    ]
    for load in loads:
        load.start()

    padded[:, :half] = before_ref[...]
    padded[:, half : half + rows] = cur_ref[...]
    padded[:, half + rows :] = after_ref[...]

    loads[0].wait()
    probe_re = probe_ref[0]
    probe_im = probe_ref[1]
    for k in range(count):
        where, row_shift, col_shift = places(row_ref, col_ref, k, side, lanes)
        row_back = lax.rem(side + 8 - row_shift, side + 8)
        col_back = lax.rem(2 * side - col_shift, 2 * side)
        for c in range(2):
            block = padded[(c,) + where]
            block = pltpu.roll(block, col_back, 1)[:, :side]
            objects[k, c] = pltpu.roll(block, row_back, 0)[:side]
        o_re = objects[k, 0]
        o_im = objects[k, 1]
        here = slice(k * side, (k + 1) * side)
        tall[:side, here] = probe_re * o_re - probe_im * o_im
        tall[side:, here] = probe_re * o_im + probe_im * o_re

    def turned(ref):
        top = jnp.concatenate([ref[:side, :side], ref[side:, :side]], axis=1)
        bottom = jnp.concatenate([ref[:side, side:], ref[side:, side:]], axis=1)
        return jnp.concatenate([top, bottom], axis=0)

    loads[1].wait()
    loads[2].wait()
    table = (high_ref[...], low_ref[...])
    flipped = (turned(high_ref), turned(low_ref))

    left = dot3(table, split(tall[...]))
    for k in range(count):
        here = slice(k * side, (k + 1) * side)
        wide[here, :side] = left[:side, here]
        wide[here, side:] = left[side:, here]
    spec = dot3(split(wide[...]), flipped)
    loads[3].wait()
    for k in range(count):
        here = slice(k * side, (k + 1) * side)
        s_re = spec[here, :side]
        s_im = spec[here, side:]
        norm = lax.rsqrt(jnp.maximum(s_re * s_re + s_im * s_im, 1.0))
        factor = 1.0 - amp_ref[k] * norm
        tall[:side, here] = s_re * factor
        tall[side:, here] = s_im * factor
    left = dot3(flipped, split(tall[...]))
    for k in range(count):
        here = slice(k * side, (k + 1) * side)
        wide[here, :side] = left[:side, here]
        wide[here, side:] = left[side:, here]
    back_ref[...] = dot3(split(wide[...]), table)

    sums = [jnp.zeros((side, side), F32)] * 3
    for k in range(count):
        here = slice(k * side, (k + 1) * side)
        o_re = objects[k, 0]
        o_im = objects[k, 1]
        b_re = back_ref[here, :side]
        b_im = back_ref[here, side:]
        sums[0] = sums[0] + (o_re * b_re + o_im * b_im)
        sums[1] = sums[1] + (o_re * b_im - o_im * b_re)
        sums[2] = sums[2] + (o_re * o_re + o_im * o_im)
    for j in range(3):
        term_ref[pl.ds(j, side, stride=3), :] = sums[j]


def deposit_kernel(
    row_ref, col_ref, cur_ref, probe_ref, back_ref, own_ref, up_ref, down_ref, grad
):
    side = probe_ref.shape[-1]
    half = side // 2
    rows = cur_ref.shape[1]
    lanes = cur_ref.shape[2]
    count = back_ref.shape[0] // side
    grad[...] = jnp.zeros(grad.shape, F32)
    probe_re = probe_ref[0]
    probe_im = probe_ref[1]
    for k in range(count):
        here = slice(k * side, (k + 1) * side)
        b_re = back_ref[here, :side]
        b_im = back_ref[here, side:]
        where, row_shift, col_shift = places(row_ref, col_ref, k, side, lanes)
        pair = (probe_re * b_re + probe_im * b_im, probe_re * b_im - probe_im * b_re)
        for c in range(2):
            block = jnp.concatenate([pair[c], jnp.zeros((8, side), F32)], axis=0)
            block = pltpu.roll(block, row_shift, 0)
            block = jnp.concatenate([block, jnp.zeros((side + 8, side), F32)], axis=1)
            block = pltpu.roll(block, col_shift, 1)
            grad[(c,) + where] = grad[(c,) + where] + block
    up_ref[...] = grad[:, :half]
    down_ref[...] = grad[:, half + rows :]
    own_ref[...] = cur_ref[...] - STEP_SIZE * grad[:, half : half + rows]


def update_kernel(own_ref, above_ref, below_ref, dh_ref, dl_ref, updated_ref, send_ref, whole, sheet):
    half = above_ref.shape[1]
    rows = own_ref.shape[1]
    per = dh_ref.shape[1]
    pieces = send_ref.shape[0] // (rows // 2)
    whole[:, half : rows - half] = own_ref[:, half : rows - half]
    whole[:, :half] = own_ref[:, :half] - STEP_SIZE * above_ref[...]
    whole[:, rows - half :] = own_ref[:, rows - half :] - STEP_SIZE * below_ref[...]
    updated_ref[...] = whole[...]
    table = (dh_ref[...], dl_ref[...])
    for c in range(2):
        product = dot3(split(whole[c]), table)
        for part in range(per // 128):
            sheet[part] = product[:, part * 128 : (part + 1) * 128]
        for s in range(2):
            for part in range(per // 128):
                piece = (2 * c + s) * (per // 128) + part
                rows_of = pl.ds(piece, rows // 2, stride=pieces)
                send_ref[rows_of, :] = sheet[part, pl.ds(s, rows // 2, stride=2), :]


def fold_kernel(share_ref, fold_ref):
    count = share_ref.shape[0] // 3
    fold_ref[...] = jnp.zeros(fold_ref.shape, F32)
    for j in range(3):
        total = jnp.sum(share_ref[pl.ds(j, count, stride=3), :], axis=0, keepdims=True)
        for t in range(fold_ref.shape[0] // 4):
            fold_ref[4 * t + j : 4 * t + j + 1, :] = total


def line_kernel(fold_ref, packed_ref, sent_ref):
    del packed_ref
    sums = [fold_ref[j : j + 1, :] for j in range(3)]
    for t in range(1, fold_ref.shape[0] // 4):
        for j in range(3):
            sums[j] = sums[j] + fold_ref[4 * t + j : 4 * t + j + 1, :]
    scale = lax.rsqrt(sums[2] + EPSILON)
    peers = fold_ref.shape[1]
    pieces = sent_ref.shape[0] // peers
    for j in range(2):
        line = jnp.broadcast_to(sums[j] * scale, (peers, peers))
        sent_ref[pl.ds(pieces - 2 + j, peers, stride=pieces), :] = line


def volume_kernel(arrived_ref, ah_ref, al_ref, volume_ref, direction_ref):
    parts = volume_ref.shape[-1] // 128
    angles = ah_ref.shape[1]
    pieces = arrived_ref.shape[0] // angles
    table = (ah_ref[...], al_ref[...])
    for c in range(2):
        direction_ref[c] = arrived_ref[pl.ds(pieces - 2 + c, angles, stride=pieces), :]
        for s in range(2):
            blocks = [
                arrived_ref[pl.ds((2 * c + s) * parts + part, angles, stride=pieces), :]
                for part in range(parts)
            ]
            volume_ref[c, s] = dot3(table, split(jnp.concatenate(blocks, axis=1)))


def band(offset, weight, length):
    column = lax.broadcasted_iota(jnp.int32, (length, offset.shape[1]), 0)
    matrix = jnp.zeros(column.shape, F32)
    for step in range(weight.shape[0]):
        matrix = jnp.where(column == offset + step, weight[step : step + 1], matrix)
    return matrix


def band_kernel(do_ref, dw_ref, ao_ref, aw_ref, dh_ref, dl_ref, ah_ref, al_ref):
    dh_ref[...], dl_ref[...] = split(band(do_ref[...], dw_ref[...], dh_ref.shape[0]))
    turned = band(ao_ref[...], aw_ref[...], ah_ref.shape[1])
    ah_ref[...], al_ref[...] = split(turned.T)


def held(value):
    return pltpu.with_memory_space_constraint(value, pltpu.VMEM)


def stay(value):
    return pltpu.with_memory_space_constraint(value, pltpu.HBM)


def vmem(count):
    return [pl.BlockSpec(memory_space=pltpu.VMEM)] * count


def local(
    projection, probe, amplitude, pos_row, pos_col, ang_offset, ang_weight, det_offset, det_weight
):
    side = probe.shape[-1]
    half = side // 2
    rows = projection.shape[2]
    lanes = projection.shape[3]
    count = amplitude.shape[1]
    angles = lax.axis_size("angle")
    tiles = lax.axis_size("tile")
    radial = det_offset.shape[0]
    up = [(i, i + 1) for i in range(tiles - 1)]
    down = [(i + 1, i) for i in range(tiles - 1)]

    current = projection[:, 0]
    shape = jax.ShapeDtypeStruct
    before = lax.ppermute(current[:, rows - half :], "tile", up)
    after = lax.ppermute(current[:, :half], "tile", down)

    regular = ang_offset.shape[0]
    det_high, det_low, ang_high, ang_low = pl.pallas_call(
        band_kernel,
        out_shape=(pltpu.VMEM((lanes, radial), BF16),) * 2
        + (pltpu.VMEM((regular, angles), BF16),) * 2,
        in_specs=vmem(4),
        out_specs=tuple(vmem(4)),
        name="bands",
        compiler_params=pltpu.CompilerParams(vmem_limit_bytes=8 << 20),
    )(det_offset[None], det_weight.T, ang_offset[None], ang_weight.T)

    high, low = complex_table(side)
    here = held(current)
    terms, back = pl.pallas_call(
        terms_kernel,
        out_shape=(pltpu.VMEM((3 * side, side), F32), pltpu.VMEM((count * side, 2 * side), F32)),
        in_specs=[pl.BlockSpec(memory_space=pltpu.SMEM)] * 2
        + vmem(3)
        + [pl.BlockSpec(memory_space=pltpu.HBM)] * 4,
        out_specs=tuple(vmem(2)),
        scratch_shapes=[
            pltpu.VMEM((2, rows + 2 * half, lanes), F32),
            pltpu.VMEM((count, 2, side, side), F32),
            pltpu.VMEM((2 * side, count * side), F32),
            pltpu.VMEM((count * side, 2 * side), F32),
            pltpu.VMEM((2, side, side), F32),
            pltpu.VMEM((count, side, side), F32),
            pltpu.VMEM((2 * side, 2 * side), BF16),
            pltpu.VMEM((2 * side, 2 * side), BF16),
            pltpu.SemaphoreType.DMA((4,)),
        ],
        name="terms",
        compiler_params=pltpu.CompilerParams(vmem_limit_bytes=20 << 20),
    )(
        pos_row, pos_col, here, held(before), held(after), stay(probe), stay(amplitude[0]),
        stay(jnp.asarray(high)), stay(jnp.asarray(low)),
    )

    shares = lax.all_to_all(terms.reshape(side, 3 * side), "angle", 0, 0, tiled=True)

    own, upper, lower = pl.pallas_call(
        deposit_kernel,
        out_shape=(
            pltpu.VMEM((2, rows, lanes), F32),
            pltpu.VMEM((2, half, lanes), F32),
            pltpu.VMEM((2, half, lanes), F32),
        ),
        in_specs=[pl.BlockSpec(memory_space=pltpu.SMEM)] * 2 + vmem(3),
        out_specs=tuple(vmem(3)),
        scratch_shapes=[pltpu.VMEM((2, rows + 2 * half, lanes), F32)],
        name="deposit",
        compiler_params=pltpu.CompilerParams(vmem_limit_bytes=12 << 20),
    )(pos_row, pos_col, here, held(probe), held(back))

    below = lax.ppermute(upper, "tile", down)
    above = lax.ppermute(lower, "tile", up)

    peers = rows // 2
    pieces = 4 * radial // 128 + 2
    updated, packed = pl.pallas_call(
        update_kernel,
        out_shape=(shape((2, rows, lanes), F32), pltpu.VMEM((peers * pieces, 128), F32)),
        in_specs=vmem(5),
        out_specs=tuple(vmem(2)),
        scratch_shapes=[
            pltpu.VMEM((2, rows, lanes), F32),
            pltpu.VMEM((radial // 128, rows, 128), F32),
        ],
        name="update",
        compiler_params=pltpu.CompilerParams(vmem_limit_bytes=12 << 20),
    )(held(own), held(above), held(below), held(det_high), held(det_low))

    folded = pl.pallas_call(
        fold_kernel,
        out_shape=pltpu.VMEM((4 * tiles, side), F32),
        in_specs=vmem(1),
        out_specs=vmem(1)[0],
        name="fold",
        compiler_params=pltpu.CompilerParams(vmem_limit_bytes=4 << 20),
    )(held(shares.reshape(3 * angles, side)))
    merged = lax.all_to_all(folded.reshape(tiles, 4 * side), "tile", 0, 0, tiled=True)
    sent = pl.pallas_call(
        line_kernel,
        out_shape=pltpu.VMEM((peers * pieces, 128), F32),
        in_specs=vmem(2),
        out_specs=vmem(1)[0],
        input_output_aliases={1: 0},
        name="line",
        compiler_params=pltpu.CompilerParams(vmem_limit_bytes=4 << 20),
    )(held(merged.reshape(4 * tiles, side)), held(packed))

    arrived = lax.all_to_all(
        sent.reshape(peers, pieces * 128), "angle", 0, 0, tiled=True
    )

    volume, direction = pl.pallas_call(
        volume_kernel,
        out_shape=(shape((2, 2, regular, radial), F32), shape((2, side, side), F32)),
        in_specs=vmem(3),
        out_specs=tuple(vmem(2)),
        name="volume",
        compiler_params=pltpu.CompilerParams(vmem_limit_bytes=8 << 20),
    )(held(arrived.reshape(angles * pieces, 128)), held(ang_high), held(ang_low))
    return (updated[:, None], direction, volume[:, None])


def solution(mesh):
    in_specs = (
        P(None, "angle", "tile", None),
        P(),
        P("angle", "tile", None, None),
        P("angle", "tile"),
        P("angle", "tile"),
        P(),
        P(),
        P(),
        P(),
    )
    out_specs = (P(None, "angle", "tile", None), P(), P(None, "tile", "angle", None, None))
    return jax.shard_map(local, mesh=mesh, in_specs=in_specs, out_specs=out_specs, check_vma=False)
```

time: 125 us -> 113 us (0.904)
  local copies, waits for them, and re-layouts: 6 us -> 1.88 us
  Pallas kernels: 12.5 us -> 9.01 us
  starting transfers between devices: 38.8 us -> 35.9 us
  other arithmetic: 1.29 us -> 0 us
    ppermute x2 -> x0, starting transfers between devices: 6.82 us -> none  [local(): total = total + lax.ppermute(total, 'tile', pairs)]
    all_to_all x1 -> x2, starting transfers between devices: 21.8 us -> 25.7 us  [the longest x1 21.8 us: local(): lax.all_to_all(terms.reshape(side, 3 * side), 'angle', 0, 0, tiled=True)]
    all_to_all x2 -> x0, local copies, waits for them, and re-layouts: 2.52 us -> none  [the longest x1 1.85 us: local(): shares = lax.all_to_all(terms, 'angle', 0, 0, tiled=True)]
    pallas_call x3 -> x6, Pallas kernels: 10.3 us -> 7.86 us  [the longest x1 4.32 us: local(): pl.pallas_call(terms_kernel, out_shape=(pltpu.VMEM((3 * side, side), F32)...]
    unnamed x13 -> x16, local copies, waits for them, and re-layouts: 2.4 us -> 0.72 us
    all_to_all x1 -> x2, waiting for transfers between devices: 15.6 us -> 15.8 us  [the longest x1 14.5 us: local(): lax.all_to_all(terms.reshape(side, 3 * side), 'angle', 0, 0, tiled=True)]
  transfers between devices with their start and end apart: 7 -> 6, of which waited for: 3 -> 3; matrix products, arithmetic and copies ran while one was open for 0% -> 0% of each run, Pallas kernels for 4% -> 3%
where the time goes in v3:
time: 113 us; the launch traced here: 112 us
  blocking collectives  47.7 us (42%)
  starting transfers between devices  35.9 us (32%)
  waiting for transfers between devices  16.9 us (15%)
  Pallas kernels  9.01 us (8%)
  local copies, waits for them, and re-layouts  1.88 us (2%)
    all_to_all x1, blocking collectives, local(): lax.all_to_all(sent.reshape(peers, pieces * 128), 'angle', 0, 0, tiled=True)  47.7 us
    all_to_all x1, starting transfers between devices, local(): lax.all_to_all(terms.reshape(side, 3 * side), 'angle', 0, 0, tiled=True)  21.8 us
    all_to_all x1, waiting for transfers between devices, local(): lax.all_to_all(terms.reshape(side, 3 * side), 'angle', 0, 0, tiled=True)  14.5 us
    ppermute x1, starting transfers between devices, local(): above = lax.ppermute(lower, 'tile', up)  4.59 us
    pallas_call x1, Pallas kernels, local(): pl.pallas_call(terms_kernel, out_shape=(pltpu.VMEM((3 * side, side), F32)...  4.32 us
    all_to_all x1, starting transfers between devices, local(): lax.all_to_all(folded.reshape(tiles, 4 * side), 'tile', 0, 0, tiled=True)  3.91 us
    ppermute x1, starting transfers between devices, local(): before = lax.ppermute(current[:, rows - half:], 'tile', up)  3.05 us
  transfers between devices with their start and end apart: 6, of which 3 were waited for; matrix products, arithmetic and copies ran while one was open for 0% of the time, Pallas kernels for 3%

profile of v3, /device:TPU:32, one launch (start us, length us, event | category | flops | bytes accessed | tf_op | source)
XLA Modules:
  0.0 112.2 jit_solution(6142096738810907148)
XLA Ops:
  0.6 0.0 copy-start
  0.6 1.2 %fusion = (f32[2,64,512]{2,1,0:T(8,128)S(1)}, f32[2,64,512]{2,1,0:T(8,128)S(1)}) fusion(f32[2,256,512]{2,1,0:T(8,128)} %bitcast.18), kind=kLoop, calls=%fused_computation | loop fusion | bytes 1048576 | tf_op jit(solution)/shard_map/slice | solution.py:267
  1.8 1.3 %collective-permute-start.1 = (f32[2,64,512]{2,1,0:T(8,128)S(1)}, f32[2,64,512]{2,1,0:T(8,128)S(1)}, u32[]{:S(2)}, u32[]{:S(2)}) collective-permute-start(f32[2,64,512]{2,1,0:T(8,128)S(1)} %get-tuple-element.35), channel_id=1, source_target_pairs={{1,0},{2,1},{3,2},{5,4},{6,5},{7,6},{9,8},{10,9},{11,10},{13,12},{... | collective-permute-start | bytes 786440 | tf_op jit(solution)/shard_map/ppermute | solution.py:267
  3.1 0.0 copy-start.4
  3.1 0.0 copy-start.5
  3.1 3.0 %collective-permute-start = (f32[2,64,512]{2,1,0:T(8,128)S(1)}, f32[2,64,512]{2,1,0:T(8,128)S(1)}, u32[]{:S(2)}, u32[]{:S(2)}) collective-permute-start(f32[2,64,512]{2,1,0:T(8,128)S(1)} %get-tuple-element.36), channel_id=1, source_target_pairs={{0,1},{1,2},{2,3},{4,5},{5,6},{6,7},{8,9},{9,10},{10,11},{12,13},{... | collective-permute-start | bytes 786440 | tf_op jit(solution)/shard_map/ppermute | solution.py:266
  6.2 0.0 collective-permute-done.1.after_ref
  6.2 1.1 collective-permute-done.before_ref
  7.3 0.0 copy-done
  7.3 0.0 copy-done.4
  7.3 0.0 copy-done.5
  7.3 4.3 %terms.1 = (f32[384,128]{1,0:T(8,128)}, f32[512,256]{1,0:T(8,128)S(1)}) custom-call(s32[1,4]{1,0:T(1,128)S(1)} %copy-done.4, s32[1,4]{1,0:T(1,128)S(1)} %copy-done.5, f32[2,256,512]{2,1,0:T(8,128)S(1)} %bitcast.19, f32[2,64,512]{2,1,0:T(8,128)S(1)} %collective-permute-done.before_ref, f32[2,64,512]{2,1,0:T(8,128)S(1)} %collective-permute-done.1.after_ref, ...), custom_call_target="tpu_custom_call" | custom-call | tf_op jit(solution)/shard_map/terms/pallas_call | solution.py:282
  11.6 0.0 copy-start.1
  11.7 21.8 %all-to-all-start = ((f32[128,1,384]{2,1,0:T(1,128)}), f32[128,1,384]{2,1,0:T(1,128)S(1)}, u32[]{:S(2)}, u32[]{:S(2)}) async-start(f32[128,1,384]{2,1,0:T(1,128)} %bitcast.8), calls=%async_computation | async-start | bytes 393216 | tf_op jit(solution)/shard_map/all_to_all | solution.py:307
  33.4 0.0 copy-done.1
  33.5 1.2 %deposit.1 = (f32[2,256,512]{2,1,0:T(8,128)S(1)}, f32[2,64,512]{2,1,0:T(8,128)S(1)}, f32[2,64,512]{2,1,0:T(8,128)S(1)}) custom-call(s32[1,4]{1,0:T(1,128)S(1)} %copy-done.4, s32[1,4]{1,0:T(1,128)S(1)} %copy-done.5, f32[2,256,512]{2,1,0:T(8,128)S(1)} %bitcast.20, f32[2,128,128]{2,1,0:T(8,128)S(1)} %copy-done.1, f32[512,256]{1,0:T(8,128)S(1)} %get-tuple-element.16.back_ref), custom_call_target="tpu_custom_call" | custom-call | tf_op jit(solution)/shard_map/deposit/pallas_call | solution.py:309
  34.6 4.6 %collective-permute-start.2 = (f32[2,64,512]{2,1,0:T(8,128)S(1)}, f32[2,64,512]{2,1,0:T(8,128)S(1)}, u32[]{:S(2)}, u32[]{:S(2)}) collective-permute-start(f32[2,64,512]{2,1,0:T(8,128)S(1)} %get-tuple-element.18), channel_id=1, source_target_pairs={{0,1},{1,2},{2,3},{4,5},{5,6},{6,7},{8,9},{9,10},{10,11},{12,13},{... | collective-permute-start | bytes 786440 | tf_op jit(solution)/shard_map/ppermute | solution.py:324
  39.2 1.3 %collective-permute-start.3 = (f32[2,64,512]{2,1,0:T(8,128)S(1)}, f32[2,64,512]{2,1,0:T(8,128)S(1)}, u32[]{:S(2)}, u32[]{:S(2)}) collective-permute-start(f32[2,64,512]{2,1,0:T(8,128)S(1)} %get-tuple-element.19), channel_id=1, source_target_pairs={{1,0},{2,1},{3,2},{5,4},{6,5},{7,6},{9,8},{10,9},{11,10},{13,12},{... | collective-permute-start | bytes 786440 | tf_op jit(solution)/shard_map/ppermute | solution.py:323
  40.5 14.5 %all-to-all-done = f32[128,1,384]{2,1,0:T(1,128)S(1)} async-done(((f32[128,1,384]{2,1,0:T(1,128)}), f32[128,1,384]{2,1,0:T(1,128)S(1)}, u32[]{:S(2)}, u32[]{:S(2)}) %all-to-all-start) | async-done | bytes 196640 | tf_op jit(solution)/shard_map/all_to_all | solution.py:307
  55.0 0.6 fold.1
  55.6 3.9 %all-to-all-start.1 = ((f32[4,1,512]{2,1,0:T(1,128)}), f32[4,1,512]{2,1,0:T(1,128)S(1)}, u32[]{:S(2)}, u32[]{:S(2)}) async-start(f32[4,1,512]{2,1,0:T(1,128)} %bitcast.10), calls=%async_computation.1 | async-start | bytes 16384 | tf_op jit(solution)/shard_map/all_to_all | solution.py:349
  59.5 0.0 copy-start.7
  59.5 0.7 copy-done.2
  60.2 0.0 copy-done.3
  60.2 0.0 copy-done.6
  60.2 0.5 bands.1
  60.8 0.0 collective-permute-done.2.above_ref
  60.8 0.0 collective-permute-done.3.below_ref
  60.8 1.2 %update.1 = (f32[2,256,512]{2,1,0:T(8,128)}, f32[1280,128]{1,0:T(8,128)S(1)}) custom-call(f32[2,256,512]{2,1,0:T(8,128)S(1)} %get-tuple-element.17.own_ref, f32[2,64,512]{2,1,0:T(8,128)S(1)} %collective-permute-done.2.above_ref, f32[2,64,512]{2,1,0:T(8,128)S(1)} %collective-permute-done.3.below_ref, bf16[512,256]{1,0:T(8,128)(2,1)S(1)} %get-tuple-element.20.dh_ref, ...), custom_call_target="tpu_custom_call" | custom-call | tf_op jit(solution)/shard_map/update/pallas_call | solution.py:328
  62.0 1.4 %all-to-all-done.1 = f32[4,1,512]{2,1,0:T(1,128)S(1)} async-done(((f32[4,1,512]{2,1,0:T(1,128)}), f32[4,1,512]{2,1,0:T(1,128)S(1)}, u32[]{:S(2)}, u32[]{:S(2)}) %all-to-all-start.1) | async-done | bytes 8224 | tf_op jit(solution)/shard_map/all_to_all | solution.py:349
  63.4 47.7 %all_to_all.27 = f32[128,1,1280]{2,1,0:T(1,128)S(1)} all-to-all(f32[128,1,1280]{2,1,0:T(1,128)S(1)} %bitcast.21), channel_id=1, replica_groups=mesh['angle'=128,'tile'=4] {'angle'}, dimensions={0} | all-to-all | bytes 1310720 | tf_op jit(solution)/shard_map/all_to_all | solution.py:360
  111.1 1.2 %volume.1 = (f32[2,2,128,256]{3,2,1,0:T(8,128)}, f32[2,128,128]{2,1,0:T(8,128)}) custom-call(f32[1280,128]{1,0:T(8,128)S(1)} %bitcast.22, bf16[128,128]{1,0:T(8,128)(2,1)S(1)} %get-tuple-element.25.ah_ref, bf16[128,128]{1,0:T(8,128)(2,1)S(1)} %get-tuple-element.26.al_ref), custom_call_target="tpu_custom_call" | custom-call | tf_op jit(solution)/shard_map/volume/pallas_call | solution.py:364
  (5 shorter events, 0.0 us)
Async XLA Ops:
  0.6 6.7 %copy-start = (f32[2,1,256,512]{3,2,1,0:T(8,128)S(1)}, f32[2,1,256,512]{3,2,1,0:T(8,128)}, u32[]{:S(2)}) copy-start(f32[2,1,256,512]{3,2,1,0:T(8,128)} %param.11) | copy-start | bytes 3145732
  1.8 4.4 %collective-permute-start.1 = (f32[2,64,512]{2,1,0:T(8,128)S(1)}, f32[2,64,512]{2,1,0:T(8,128)S(1)}, u32[]{:S(2)}, u32[]{:S(2)}) collective-permute-start(f32[2,64,512]{2,1,0:T(8,128)S(1)} %get-tuple-element.35), channel_id=1, source_target_pairs={{1,0},{2,1},{3,2},{5,4},{6,5},{7,6},{9,8},{10,9},{11,10},{13,12},{... | collective-permute-start | bytes 786440 | tf_op jit(solution)/shard_map/ppermute | solution.py:267
  3.1 4.2 %copy-start.4 = (s32[1,4]{1,0:T(1,128)S(1)}, s32[1,4]{1,0:T(1,128)}, u32[]{:S(2)}) copy-start(s32[1,4]{1,0:T(1,128)} %row_ref.3) | copy-start | bytes 52
  3.1 4.2 %copy-start.5 = (s32[1,4]{1,0:T(1,128)S(1)}, s32[1,4]{1,0:T(1,128)}, u32[]{:S(2)}) copy-start(s32[1,4]{1,0:T(1,128)} %col_ref.3) | copy-start | bytes 52
  3.1 4.2 %collective-permute-start = (f32[2,64,512]{2,1,0:T(8,128)S(1)}, f32[2,64,512]{2,1,0:T(8,128)S(1)}, u32[]{:S(2)}, u32[]{:S(2)}) collective-permute-start(f32[2,64,512]{2,1,0:T(8,128)S(1)} %get-tuple-element.36), channel_id=1, source_target_pairs={{0,1},{1,2},{2,3},{4,5},{5,6},{6,7},{8,9},{9,10},{10,11},{12,13},{... | collective-permute-start | bytes 786440 | tf_op jit(solution)/shard_map/ppermute | solution.py:266
  11.6 21.8 %copy-start.1 = (f32[2,128,128]{2,1,0:T(8,128)S(1)}, f32[2,128,128]{2,1,0:T(8,128)}, u32[]{:S(2)}) copy-start(f32[2,128,128]{2,1,0:T(8,128)} %probe_ref.1) | copy-start | bytes 393220
  11.7 43.3 %all-to-all-start = ((f32[128,1,384]{2,1,0:T(1,128)}), f32[128,1,384]{2,1,0:T(1,128)S(1)}, u32[]{:S(2)}, u32[]{:S(2)}) async-start(f32[128,1,384]{2,1,0:T(1,128)} %bitcast.8), calls=%async_computation | async-start | bytes 393216 | tf_op jit(solution)/shard_map/all_to_all | solution.py:307
  34.6 26.1 %collective-permute-start.2 = (f32[2,64,512]{2,1,0:T(8,128)S(1)}, f32[2,64,512]{2,1,0:T(8,128)S(1)}, u32[]{:S(2)}, u32[]{:S(2)}) collective-permute-start(f32[2,64,512]{2,1,0:T(8,128)S(1)} %get-tuple-element.18), channel_id=1, source_target_pairs={{0,1},{1,2},{2,3},{4,5},{5,6},{6,7},{8,9},{9,10},{10,11},{12,13},{... | collective-permute-start | bytes 786440 | tf_op jit(solution)/shard_map/ppermute | solution.py:324
  39.2 21.5 %collective-permute-start.3 = (f32[2,64,512]{2,1,0:T(8,128)S(1)}, f32[2,64,512]{2,1,0:T(8,128)S(1)}, u32[]{:S(2)}, u32[]{:S(2)}) collective-permute-start(f32[2,64,512]{2,1,0:T(8,128)S(1)} %get-tuple-element.19), channel_id=1, source_target_pairs={{1,0},{2,1},{3,2},{5,4},{6,5},{7,6},{9,8},{10,9},{11,10},{13,12},{... | collective-permute-start | bytes 786440 | tf_op jit(solution)/shard_map/ppermute | solution.py:323
  55.6 7.7 %all-to-all-start.1 = ((f32[4,1,512]{2,1,0:T(1,128)}), f32[4,1,512]{2,1,0:T(1,128)S(1)}, u32[]{:S(2)}, u32[]{:S(2)}) async-start(f32[4,1,512]{2,1,0:T(1,128)} %bitcast.10), calls=%async_computation.1 | async-start | bytes 16384 | tf_op jit(solution)/shard_map/all_to_all | solution.py:349
  59.5 0.7 copy-start.2
  59.5 0.7 copy-start.3
  59.5 0.7 copy-start.6
  59.5 0.7 copy-start.7

commit v4 on v3

--- a/solution.py
+++ b/solution.py
@@ -10,6 +10,7 @@
 
 STEP_SIZE = 0.1
 EPSILON = 1e-06
+LINE = 16
 F32 = jnp.float32
 BF16 = jnp.bfloat16
 
@@ -165,8 +166,8 @@
 def update_kernel(own_ref, above_ref, below_ref, dh_ref, dl_ref, updated_ref, send_ref, whole, sheet):
     half = above_ref.shape[1]
     rows = own_ref.shape[1]
-    per = dh_ref.shape[1]
-    pieces = send_ref.shape[0] // (rows // 2)
+    parts = dh_ref.shape[1] // 128
+    chunk = send_ref.shape[0] // LINE
     whole[:, half : rows - half] = own_ref[:, half : rows - half]
     whole[:, :half] = own_ref[:, :half] - STEP_SIZE * above_ref[...]
     whole[:, rows - half :] = own_ref[:, rows - half :] - STEP_SIZE * below_ref[...]
@@ -174,13 +175,24 @@
     table = (dh_ref[...], dl_ref[...])
     for c in range(2):
         product = dot3(split(whole[c]), table)
-        for part in range(per // 128):
+        for part in range(parts):
             sheet[part] = product[:, part * 128 : (part + 1) * 128]
         for s in range(2):
-            for part in range(per // 128):
-                piece = (2 * c + s) * (per // 128) + part
-                rows_of = pl.ds(piece, rows // 2, stride=pieces)
-                send_ref[rows_of, :] = sheet[part, pl.ds(s, rows // 2, stride=2), :]
+            for part in range(parts):
+                piece = (2 * c + s) * parts + part
+                for g in range(rows // 2 // LINE):
+                    source = pl.ds(2 * LINE * g + s, LINE, stride=2)
+                    target = pl.ds(4 * parts * g + piece, LINE, stride=chunk)
+                    send_ref[target, :] = sheet[part, source, :]
+
+
+def gather_kernel(share_ref, sum_ref):
+    count = share_ref.shape[0] // sum_ref.shape[0]
+    step = sum_ref.shape[0]
+    total = share_ref[:step, :]
+    for i in range(1, count):
+        total = total + share_ref[i * step : (i + 1) * step, :]
+    sum_ref[...] = total
 
 
 def fold_kernel(share_ref, fold_ref):
@@ -199,26 +211,47 @@
         for j in range(3):
             sums[j] = sums[j] + fold_ref[4 * t + j : 4 * t + j + 1, :]
     scale = lax.rsqrt(sums[2] + EPSILON)
-    peers = fold_ref.shape[1]
-    pieces = sent_ref.shape[0] // peers
+    chunk = sent_ref.shape[0] // LINE
     for j in range(2):
-        line = jnp.broadcast_to(sums[j] * scale, (peers, peers))
-        sent_ref[pl.ds(pieces - 2 + j, peers, stride=pieces), :] = line
+        line = jnp.broadcast_to(sums[j] * scale, (LINE, fold_ref.shape[1]))
+        sent_ref[pl.ds(chunk - 2 + j, LINE, stride=chunk), :] = line
+
+
+def turn_kernel(arrived_ref, sent_ref):
+    old = arrived_ref.shape[0] // LINE
+    pieces = 8
+    groups = (old - 2) // pieces
+    new = LINE * (pieces + 2)
+    for g in range(groups):
+        for j in range(pieces):
+            block = arrived_ref[pl.ds(g * pieces + j, LINE, stride=old), :]
+            sent_ref[pl.ds(g * new + j, LINE, stride=pieces), :] = block
+    for c in range(2):
+        block = arrived_ref[pl.ds(old - 2 + c, LINE, stride=old), :]
+        for g in range(groups):
+            sent_ref[pl.ds(g * new + LINE * pieces + c, LINE, stride=2), :] = block
 
 
 def volume_kernel(arrived_ref, ah_ref, al_ref, volume_ref, direction_ref):
     parts = volume_ref.shape[-1] // 128
-    angles = ah_ref.shape[1]
-    pieces = arrived_ref.shape[0] // angles
+    pieces = 4 * parts
+    groups = ah_ref.shape[1] // LINE
+    new = arrived_ref.shape[0] // groups
     table = (ah_ref[...], al_ref[...])
     for c in range(2):
-        direction_ref[c] = arrived_ref[pl.ds(pieces - 2 + c, angles, stride=pieces), :]
+        for g in range(groups):
+            source = pl.ds(g * new + LINE * pieces + c, LINE, stride=2)
+            direction_ref[c, LINE * g : LINE * (g + 1), :] = arrived_ref[source, :]
         for s in range(2):
-            blocks = [
-                arrived_ref[pl.ds((2 * c + s) * parts + part, angles, stride=pieces), :]
-                for part in range(parts)
-            ]
-            volume_ref[c, s] = dot3(table, split(jnp.concatenate(blocks, axis=1)))
+            columns = []
+            for part in range(parts):
+                piece = (2 * c + s) * parts + part
+                blocks = [
+                    arrived_ref[pl.ds(g * new + piece, LINE, stride=pieces), :]
+                    for g in range(groups)
+                ]
+                columns.append(jnp.concatenate(blocks, axis=0))
+            volume_ref[c, s] = dot3(table, split(jnp.concatenate(columns, axis=1)))
 
 
 def band(offset, weight, length):
@@ -260,6 +293,10 @@
     radial = det_offset.shape[0]
     up = [(i, i + 1) for i in range(tiles - 1)]
     down = [(i + 1, i) for i in range(tiles - 1)]
+
+    groups = angles // LINE
+    along = [[g * LINE + i for i in range(LINE)] for g in range(groups)]
+    across = [[g * LINE + i for g in range(groups)] for i in range(LINE)]
 
     current = projection[:, 0]
     shape = jax.ShapeDtypeStruct
@@ -304,7 +341,9 @@
         stay(jnp.asarray(high)), stay(jnp.asarray(low)),
     )
 
-    shares = lax.all_to_all(terms.reshape(side, 3 * side), "angle", 0, 0, tiled=True)
+    shares = lax.all_to_all(
+        terms, "angle", 0, 0, tiled=True, axis_index_groups=across
+    )
 
     own, upper, lower = pl.pallas_call(
         deposit_kernel,
@@ -323,11 +362,23 @@
     below = lax.ppermute(upper, "tile", down)
     above = lax.ppermute(lower, "tile", up)
 
-    peers = rows // 2
-    pieces = 4 * radial // 128 + 2
+    gathered = pl.pallas_call(
+        gather_kernel,
+        out_shape=pltpu.VMEM((3 * LINE, side), F32),
+        in_specs=vmem(1),
+        out_specs=vmem(1)[0],
+        name="gather",
+        compiler_params=pltpu.CompilerParams(vmem_limit_bytes=4 << 20),
+    )(held(shares))
+    seconds = lax.all_to_all(
+        gathered.reshape(LINE, 3 * side), "angle", 0, 0, tiled=True, axis_index_groups=along
+    )
+
+    pieces = 4 * radial // 128
+    chunk = groups * pieces + 2
     updated, packed = pl.pallas_call(
         update_kernel,
-        out_shape=(shape((2, rows, lanes), F32), pltpu.VMEM((peers * pieces, 128), F32)),
+        out_shape=(shape((2, rows, lanes), F32), pltpu.VMEM((LINE * chunk, 128), F32)),
         in_specs=vmem(5),
         out_specs=tuple(vmem(2)),
         scratch_shapes=[
@@ -345,11 +396,11 @@
         out_specs=vmem(1)[0],
         name="fold",
         compiler_params=pltpu.CompilerParams(vmem_limit_bytes=4 << 20),
-    )(held(shares.reshape(3 * angles, side)))
+    )(held(seconds.reshape(3 * LINE, side)))
     merged = lax.all_to_all(folded.reshape(tiles, 4 * side), "tile", 0, 0, tiled=True)
     sent = pl.pallas_call(
         line_kernel,
-        out_shape=pltpu.VMEM((peers * pieces, 128), F32),
+        out_shape=pltpu.VMEM((LINE * chunk, 128), F32),
         in_specs=vmem(2),
         out_specs=vmem(1)[0],
         input_output_aliases={1: 0},
@@ -358,8 +409,18 @@
     )(held(merged.reshape(4 * tiles, side)), held(packed))
 
     arrived = lax.all_to_all(
-        sent.reshape(peers, pieces * 128), "angle", 0, 0, tiled=True
-    )
+        sent.reshape(LINE, chunk * 128), "angle", 0, 0, tiled=True, axis_index_groups=along
+    )
+    block = LINE * (pieces + 2)
+    turned = pl.pallas_call(
+        turn_kernel,
+        out_shape=pltpu.VMEM((groups * block, 128), F32),
+        in_specs=vmem(1),
+        out_specs=vmem(1)[0],
+        name="turn",
+        compiler_params=pltpu.CompilerParams(vmem_limit_bytes=4 << 20),
+    )(held(arrived.reshape(LINE * chunk, 128)))
+    landed = lax.all_to_all(turned, "angle", 0, 0, tiled=True, axis_index_groups=across)
 
     volume, direction = pl.pallas_call(
         volume_kernel,
@@ -368,7 +429,7 @@
         out_specs=tuple(vmem(2)),
         name="volume",
         compiler_params=pltpu.CompilerParams(vmem_limit_bytes=8 << 20),
-    )(held(arrived.reshape(angles * pieces, 128)), held(ang_high), held(ang_low))
+    )(held(landed), held(ang_high), held(ang_low))
     return (updated[:, None], direction, volume[:, None])
 
 

time: 113 us -> 122 us (1.080)
  the two profiles are of different devices: /device:TPU:32 before, /device:TPU:2 now
where the time goes in v4:
time: 122 us; the launch traced here: 121 us
  blocking collectives  81.4 us (67%)
  starting transfers between devices  16.7 us (14%)
  waiting for transfers between devices  11.1 us (9%)
  Pallas kernels  9.15 us (8%)
  local copies, waits for them, and re-layouts  1.88 us (2%)
    all_to_all x1, blocking collectives, local(): lax.all_to_all(sent.reshape(LINE, chunk * 128), 'angle', 0, 0, tiled=True...  37.1 us
    all_to_all x1, blocking collectives, local(): lax.all_to_all(gathered.reshape(LINE, 3 * side), 'angle', 0, 0, tiled=Tru...  26.3 us
    all_to_all x1, blocking collectives, local(): lax.all_to_all(turned, 'angle', 0, 0, tiled=True, axis_index_groups=across)  18 us
    ppermute x1, waiting for transfers between devices, local(): before = lax.ppermute(current[:, rows - half:], 'tile', up)  8.1 us
    pallas_call x1, Pallas kernels, local(): pl.pallas_call(terms_kernel, out_shape=(pltpu.VMEM((3 * side, side), F32)...  4.34 us
    ppermute x1, starting transfers between devices, local(): below = lax.ppermute(upper, 'tile', down)  3.64 us
    all_to_all x1, starting transfers between devices, local(): lax.all_to_all(terms, 'angle', 0, 0, tiled=True, axis_index_groups=across)  3.54 us
    all_to_all x1, starting transfers between devices, local(): lax.all_to_all(folded.reshape(tiles, 4 * side), 'tile', 0, 0, tiled=True)  3.29 us
  transfers between devices with their start and end apart: 6, of which 3 were waited for; matrix products, arithmetic and copies ran while one was open for 0% of the time, Pallas kernels for 3%

profile of v4, /device:TPU:2, one launch (start us, length us, event | category | flops | bytes accessed | tf_op | source)
XLA Modules:
  0.0 121.1 jit_solution(17377594540312860046)
XLA Ops:
  0.6 0.0 copy-start
  0.6 1.2 fusion
  1.8 1.9 %collective-permute-start.1 = (f32[2,64,512]{2,1,0:T(8,128)S(1)}, f32[2,64,512]{2,1,0:T(8,128)S(1)}, u32[]{:S(2)}, u32[]{:S(2)}) collective-permute-start(f32[2,64,512]{2,1,0:T(8,128)S(1)} %get-tuple-element.35), channel_id=1, source_target_pairs={{1,0},{2,1},{3,2},{5,4},{6,5},{7,6},{9,8},{10,9},{11,10},{13,12},{... | collective-permute-start | bytes 786440 | tf_op jit(solution)/shard_map/ppermute | solution.py:304
  3.7 0.0 copy-start.4
  3.7 0.0 copy-start.5
  3.8 2.4 %collective-permute-start = (f32[2,64,512]{2,1,0:T(8,128)S(1)}, f32[2,64,512]{2,1,0:T(8,128)S(1)}, u32[]{:S(2)}, u32[]{:S(2)}) collective-permute-start(f32[2,64,512]{2,1,0:T(8,128)S(1)} %get-tuple-element.36), channel_id=1, source_target_pairs={{0,1},{1,2},{2,3},{4,5},{5,6},{6,7},{8,9},{9,10},{10,11},{12,13},{... | collective-permute-start | bytes 786440 | tf_op jit(solution)/shard_map/ppermute | solution.py:303
  6.2 1.4 %collective-permute-done.1.after_ref = f32[2,64,512]{2,1,0:T(8,128)S(1)} collective-permute-done((f32[2,64,512]{2,1,0:T(8,128)S(1)}, f32[2,64,512]{2,1,0:T(8,128)S(1)}, u32[]{:S(2)}, u32[]{:S(2)}) %collective-permute-start.1) | collective-permute-done | bytes 262176 | tf_op jit(solution)/shard_map/ppermute | solution.py:304
  7.6 8.1 %collective-permute-done.before_ref = f32[2,64,512]{2,1,0:T(8,128)S(1)} collective-permute-done((f32[2,64,512]{2,1,0:T(8,128)S(1)}, f32[2,64,512]{2,1,0:T(8,128)S(1)}, u32[]{:S(2)}, u32[]{:S(2)}) %collective-permute-start) | collective-permute-done | bytes 262176 | tf_op jit(solution)/shard_map/ppermute | solution.py:303
  15.7 0.0 copy-done
  15.7 0.0 copy-done.4
  15.7 4.3 %terms.1 = (f32[384,128]{1,0:T(8,128)}, f32[512,256]{1,0:T(8,128)S(1)}) custom-call(s32[1,4]{1,0:T(1,128)S(1)} %copy-done.4, s32[1,4]{1,0:T(1,128)S(1)} %copy-done.5, f32[2,256,512]{2,1,0:T(8,128)S(1)} %bitcast.23, f32[2,64,512]{2,1,0:T(8,128)S(1)} %collective-permute-done.before_ref, f32[2,64,512]{2,1,0:T(8,128)S(1)} %collective-permute-done.1.after_ref, ...), custom_call_target="tpu_custom_call" | custom-call | tf_op jit(solution)/shard_map/terms/pallas_call | solution.py:319
  20.0 0.0 copy-start.1
  20.1 3.5 %all-to-all-start = ((f32[8,48,128]{2,1,0:T(8,128)}), f32[8,48,128]{2,1,0:T(8,128)S(1)}, u32[]{:S(2)}, u32[]{:S(2)}) async-start(f32[8,48,128]{2,1,0:T(8,128)} %bitcast.8), calls=%async_computation | async-start | bytes 393216 | tf_op jit(solution)/shard_map/all_to_all | solution.py:344
  23.6 1.2 deposit.1
  24.8 1.9 %collective-permute-start.2 = (f32[2,64,512]{2,1,0:T(8,128)S(1)}, f32[2,64,512]{2,1,0:T(8,128)S(1)}, u32[]{:S(2)}, u32[]{:S(2)}) collective-permute-start(f32[2,64,512]{2,1,0:T(8,128)S(1)} %get-tuple-element.18), channel_id=1, source_target_pairs={{0,1},{1,2},{2,3},{4,5},{5,6},{6,7},{8,9},{9,10},{10,11},{12,13},{... | collective-permute-start | bytes 786440 | tf_op jit(solution)/shard_map/ppermute | solution.py:363
  26.7 3.6 %collective-permute-start.3 = (f32[2,64,512]{2,1,0:T(8,128)S(1)}, f32[2,64,512]{2,1,0:T(8,128)S(1)}, u32[]{:S(2)}, u32[]{:S(2)}) collective-permute-start(f32[2,64,512]{2,1,0:T(8,128)S(1)} %get-tuple-element.19), channel_id=1, source_target_pairs={{1,0},{2,1},{3,2},{5,4},{6,5},{7,6},{9,8},{10,9},{11,10},{13,12},{... | collective-permute-start | bytes 786440 | tf_op jit(solution)/shard_map/ppermute | solution.py:362
  30.4 1.6 %all-to-all-done = f32[8,48,128]{2,1,0:T(8,128)S(1)} async-done(((f32[8,48,128]{2,1,0:T(8,128)}), f32[8,48,128]{2,1,0:T(8,128)S(1)}, u32[]{:S(2)}, u32[]{:S(2)}) %all-to-all-start) | async-done | bytes 196640 | tf_op jit(solution)/shard_map/all_to_all | solution.py:344
  32.0 26.3 %all_to_all.49 = f32[16,1,384]{2,1,0:T(1,128)S(1)} all-to-all(f32[16,1,384]{2,1,0:T(1,128)S(1)} %bitcast.30), channel_id=1, replica_groups={{0,4,8,12,16,20,24,28,32,36,40,44,48,52,56,60},{64,68,72,76,80,84,88,92..., dimensions={0} | all-to-all | bytes 49152 | tf_op jit(solution)/shard_map/all_to_all | solution.py:373
  58.3 0.6 fold.1
  58.9 3.3 %all-to-all-start.2 = ((f32[4,1,512]{2,1,0:T(1,128)}), f32[4,1,512]{2,1,0:T(1,128)S(1)}, u32[]{:S(2)}, u32[]{:S(2)}) async-start(f32[4,1,512]{2,1,0:T(1,128)} %bitcast.12), calls=%async_computation.2 | async-start | bytes 16384 | tf_op jit(solution)/shard_map/all_to_all | solution.py:400
  62.2 0.7 copy-done.2
  62.9 0.0 copy-done.3
  62.9 0.0 copy-done.6
  62.9 0.5 bands.1
  63.4 0.0 collective-permute-done.2.above_ref
  63.4 0.0 collective-permute-done.3.below_ref
  63.5 1.2 update.1
  64.6 0.0 all-to-all-done.2
  64.7 37.1 %all_to_all.50 = f32[16,1,8448]{2,1,0:T(1,128)S(1)} all-to-all(f32[16,1,8448]{2,1,0:T(1,128)S(1)} %bitcast.27), channel_id=1, replica_groups={{0,4,8,12,16,20,24,28,32,36,40,44,48,52,56,60},{64,68,72,76,80,84,88,92..., dimensions={0} | all-to-all | bytes 1081344 | tf_op jit(solution)/shard_map/all_to_all | solution.py:411
  101.7 0.1 turn.1
  101.8 18.0 %all_to_all.51 = f32[8,160,128]{2,1,0:T(8,128)S(1)} all-to-all(f32[8,160,128]{2,1,0:T(8,128)S(1)} %bitcast.26), channel_id=1, replica_groups={{0,64,128,192,256,320,384,448},{4,68,132,196,260,324,388,452},{8,72,136..., dimensions={0} | all-to-all | bytes 1310720 | tf_op jit(solution)/shard_map/all_to_all | solution.py:423
  119.9 1.2 volume.1
  (9 shorter events, 0.0 us)
Async XLA Ops:
  0.6 15.1 %copy-start = (f32[2,1,256,512]{3,2,1,0:T(8,128)S(1)}, f32[2,1,256,512]{3,2,1,0:T(8,128)}, u32[]{:S(2)}) copy-start(f32[2,1,256,512]{3,2,1,0:T(8,128)} %param.11) | copy-start | bytes 3145732
  1.8 5.8 %collective-permute-start.1 = (f32[2,64,512]{2,1,0:T(8,128)S(1)}, f32[2,64,512]{2,1,0:T(8,128)S(1)}, u32[]{:S(2)}, u32[]{:S(2)}) collective-permute-start(f32[2,64,512]{2,1,0:T(8,128)S(1)} %get-tuple-element.35), channel_id=1, source_target_pairs={{1,0},{2,1},{3,2},{5,4},{6,5},{7,6},{9,8},{10,9},{11,10},{13,12},{... | collective-permute-start | bytes 786440 | tf_op jit(solution)/shard_map/ppermute | solution.py:304
  3.7 12.0 %copy-start.4 = (s32[1,4]{1,0:T(1,128)S(1)}, s32[1,4]{1,0:T(1,128)}, u32[]{:S(2)}) copy-start(s32[1,4]{1,0:T(1,128)} %row_ref.3) | copy-start | bytes 52
  3.7 12.0 %copy-start.5 = (s32[1,4]{1,0:T(1,128)S(1)}, s32[1,4]{1,0:T(1,128)}, u32[]{:S(2)}) copy-start(s32[1,4]{1,0:T(1,128)} %col_ref.3) | copy-start | bytes 52
  3.8 11.9 %collective-permute-start = (f32[2,64,512]{2,1,0:T(8,128)S(1)}, f32[2,64,512]{2,1,0:T(8,128)S(1)}, u32[]{:S(2)}, u32[]{:S(2)}) collective-permute-start(f32[2,64,512]{2,1,0:T(8,128)S(1)} %get-tuple-element.36), channel_id=1, source_target_pairs={{0,1},{1,2},{2,3},{4,5},{5,6},{6,7},{8,9},{9,10},{10,11},{12,13},{... | collective-permute-start | bytes 786440 | tf_op jit(solution)/shard_map/ppermute | solution.py:303
  20.0 3.6 %copy-start.1 = (f32[2,128,128]{2,1,0:T(8,128)S(1)}, f32[2,128,128]{2,1,0:T(8,128)}, u32[]{:S(2)}) copy-start(f32[2,128,128]{2,1,0:T(8,128)} %probe_ref.1) | copy-start | bytes 393220
  20.1 11.9 %all-to-all-start = ((f32[8,48,128]{2,1,0:T(8,128)}), f32[8,48,128]{2,1,0:T(8,128)S(1)}, u32[]{:S(2)}, u32[]{:S(2)}) async-start(f32[8,48,128]{2,1,0:T(8,128)} %bitcast.8), calls=%async_computation | async-start | bytes 393216 | tf_op jit(solution)/shard_map/all_to_all | solution.py:344
  24.8 38.6 %collective-permute-start.2 = (f32[2,64,512]{2,1,0:T(8,128)S(1)}, f32[2,64,512]{2,1,0:T(8,128)S(1)}, u32[]{:S(2)}, u32[]{:S(2)}) collective-permute-start(f32[2,64,512]{2,1,0:T(8,128)S(1)} %get-tuple-element.18), channel_id=1, source_target_pairs={{0,1},{1,2},{2,3},{4,5},{5,6},{6,7},{8,9},{9,10},{10,11},{12,13},{... | collective-permute-start | bytes 786440 | tf_op jit(solution)/shard_map/ppermute | solution.py:363
  26.7 36.7 %collective-permute-start.3 = (f32[2,64,512]{2,1,0:T(8,128)S(1)}, f32[2,64,512]{2,1,0:T(8,128)S(1)}, u32[]{:S(2)}, u32[]{:S(2)}) collective-permute-start(f32[2,64,512]{2,1,0:T(8,128)S(1)} %get-tuple-element.19), channel_id=1, source_target_pairs={{1,0},{2,1},{3,2},{5,4},{6,5},{7,6},{9,8},{10,9},{11,10},{13,12},{... | collective-permute-start | bytes 786440 | tf_op jit(solution)/shard_map/ppermute | solution.py:362
  58.9 5.7 %all-to-all-start.2 = ((f32[4,1,512]{2,1,0:T(1,128)}), f32[4,1,512]{2,1,0:T(1,128)S(1)}, u32[]{:S(2)}, u32[]{:S(2)}) async-start(f32[4,1,512]{2,1,0:T(1,128)} %bitcast.12), calls=%async_computation.2 | async-start | bytes 16384 | tf_op jit(solution)/shard_map/all_to_all | solution.py:400
  62.2 0.7 copy-start.2
  62.2 0.7 copy-start.3
  62.2 0.7 copy-start.6
  62.2 0.7 copy-start.7

commit v5 on v3

--- a/solution.py
+++ b/solution.py
@@ -10,6 +10,7 @@
 
 STEP_SIZE = 0.1
 EPSILON = 1e-06
+LINE = 16
 F32 = jnp.float32
 BF16 = jnp.bfloat16
 
@@ -183,6 +184,15 @@
                 send_ref[rows_of, :] = sheet[part, pl.ds(s, rows // 2, stride=2), :]
 
 
+def gather_kernel(share_ref, sum_ref):
+    count = share_ref.shape[0] // sum_ref.shape[0]
+    step = sum_ref.shape[0]
+    total = share_ref[:step, :]
+    for i in range(1, count):
+        total = total + share_ref[i * step : (i + 1) * step, :]
+    sum_ref[...] = total
+
+
 def fold_kernel(share_ref, fold_ref):
     count = share_ref.shape[0] // 3
     fold_ref[...] = jnp.zeros(fold_ref.shape, F32)
@@ -260,6 +270,10 @@
     radial = det_offset.shape[0]
     up = [(i, i + 1) for i in range(tiles - 1)]
     down = [(i + 1, i) for i in range(tiles - 1)]
+
+    groups = angles // LINE
+    across = [[g * LINE + i for g in range(groups)] for i in range(LINE)]
+    along = [[g * LINE + i for i in range(LINE)] for g in range(groups)]
 
     current = projection[:, 0]
     shape = jax.ShapeDtypeStruct
@@ -304,7 +318,9 @@
         stay(jnp.asarray(high)), stay(jnp.asarray(low)),
     )
 
-    shares = lax.all_to_all(terms.reshape(side, 3 * side), "angle", 0, 0, tiled=True)
+    shares = lax.all_to_all(
+        terms, "angle", 0, 0, tiled=True, axis_index_groups=across
+    )
 
     own, upper, lower = pl.pallas_call(
         deposit_kernel,
@@ -322,6 +338,18 @@
 
     below = lax.ppermute(upper, "tile", down)
     above = lax.ppermute(lower, "tile", up)
+
+    gathered = pl.pallas_call(
+        gather_kernel,
+        out_shape=pltpu.VMEM((3 * LINE, side), F32),
+        in_specs=vmem(1),
+        out_specs=vmem(1)[0],
+        name="gather",
+        compiler_params=pltpu.CompilerParams(vmem_limit_bytes=4 << 20),
+    )(held(shares))
+    seconds = lax.all_to_all(
+        gathered.reshape(LINE, 3 * side), "angle", 0, 0, tiled=True, axis_index_groups=along
+    )
 
     peers = rows // 2
     pieces = 4 * radial // 128 + 2
@@ -345,7 +373,7 @@
         out_specs=vmem(1)[0],
         name="fold",
         compiler_params=pltpu.CompilerParams(vmem_limit_bytes=4 << 20),
-    )(held(shares.reshape(3 * angles, side)))
+    )(held(seconds.reshape(3 * LINE, side)))
     merged = lax.all_to_all(folded.reshape(tiles, 4 * side), "tile", 0, 0, tiled=True)
     sent = pl.pallas_call(
         line_kernel,

time: 113 us -> 116 us (1.027)
  blocking collectives: 47.7 us -> 76.4 us
  waiting for transfers between devices: 16.9 us -> 3.59 us
  starting transfers between devices: 35.9 us -> 23.8 us
    all_to_all x0 -> x1, blocking collectives: none -> 26.4 us  [local(): lax.all_to_all(gathered.reshape(LINE, 3 * side), 'angle', 0, 0, tiled=Tru...]
    all_to_all x1, starting transfers between devices: 21.8 us -> 7.07 us  [local(): lax.all_to_all(terms, 'angle', 0, 0, tiled=True, axis_index_groups=across)]
    all_to_all x1, waiting for transfers between devices: 14.5 us -> 1.09 us  [local(): lax.all_to_all(terms, 'angle', 0, 0, tiled=True, axis_index_groups=across)]
    all_to_all x1, starting transfers between devices: 3.91 us -> 6.26 us  [local(): lax.all_to_all(folded.reshape(tiles, 4 * side), 'tile', 0, 0, tiled=True)]
    all_to_all x1, blocking collectives: 47.7 us -> 50 us  [local(): lax.all_to_all(sent.reshape(peers, pieces * 128), 'angle', 0, 0, tiled=True)]
where the time goes in v5:
time: 116 us; the launch traced here: 115 us
  blocking collectives  76.4 us (66%)
  starting transfers between devices  23.8 us (21%)
  Pallas kernels  9.01 us (8%)
  waiting for transfers between devices  3.59 us (3%)
  local copies, waits for them, and re-layouts  1.88 us (2%)
    all_to_all x1, blocking collectives, local(): lax.all_to_all(sent.reshape(peers, pieces * 128), 'angle', 0, 0, tiled=True)  50 us
    all_to_all x1, blocking collectives, local(): lax.all_to_all(gathered.reshape(LINE, 3 * side), 'angle', 0, 0, tiled=Tru...  26.4 us
    all_to_all x1, starting transfers between devices, local(): lax.all_to_all(terms, 'angle', 0, 0, tiled=True, axis_index_groups=across)  7.07 us
    all_to_all x1, starting transfers between devices, local(): lax.all_to_all(folded.reshape(tiles, 4 * side), 'tile', 0, 0, tiled=True)  6.26 us
    ppermute x1, starting transfers between devices, local(): above = lax.ppermute(lower, 'tile', up)  4.87 us
    pallas_call x1, Pallas kernels, local(): pl.pallas_call(terms_kernel, out_shape=(pltpu.VMEM((3 * side, side), F32)...  4.32 us
    ppermute x1, starting transfers between devices, local(): before = lax.ppermute(current[:, rows - half:], 'tile', up)  3.05 us
  transfers between devices with their start and end apart: 6, of which 3 were waited for; matrix products, arithmetic and copies ran while one was open for 0% of the time, Pallas kernels for 3%

profile of v5, /device:TPU:32, one launch (start us, length us, event | category | flops | bytes accessed | tf_op | source)
XLA Modules:
  0.0 115.4 jit_solution(4387920346968676611)
XLA Ops:
  0.6 0.0 copy-start
  0.6 1.2 %fusion = (f32[2,64,512]{2,1,0:T(8,128)S(1)}, f32[2,64,512]{2,1,0:T(8,128)S(1)}) fusion(f32[2,256,512]{2,1,0:T(8,128)} %bitcast.20), kind=kLoop, calls=%fused_computation | loop fusion | bytes 1048576 | tf_op jit(solution)/shard_map/slice | solution.py:281
  1.8 1.3 %collective-permute-start.1 = (f32[2,64,512]{2,1,0:T(8,128)S(1)}, f32[2,64,512]{2,1,0:T(8,128)S(1)}, u32[]{:S(2)}, u32[]{:S(2)}) collective-permute-start(f32[2,64,512]{2,1,0:T(8,128)S(1)} %get-tuple-element.35), channel_id=1, source_target_pairs={{1,0},{2,1},{3,2},{5,4},{6,5},{7,6},{9,8},{10,9},{11,10},{13,12},{... | collective-permute-start | bytes 786440 | tf_op jit(solution)/shard_map/ppermute | solution.py:281
  3.1 0.0 copy-start.4
  3.1 0.0 copy-start.5
  3.1 3.0 %collective-permute-start = (f32[2,64,512]{2,1,0:T(8,128)S(1)}, f32[2,64,512]{2,1,0:T(8,128)S(1)}, u32[]{:S(2)}, u32[]{:S(2)}) collective-permute-start(f32[2,64,512]{2,1,0:T(8,128)S(1)} %get-tuple-element.36), channel_id=1, source_target_pairs={{0,1},{1,2},{2,3},{4,5},{5,6},{6,7},{8,9},{9,10},{10,11},{12,13},{... | collective-permute-start | bytes 786440 | tf_op jit(solution)/shard_map/ppermute | solution.py:280
  6.2 0.0 collective-permute-done.1.after_ref
  6.2 1.1 collective-permute-done.before_ref
  7.3 0.0 copy-done
  7.3 0.0 copy-done.4
  7.3 4.3 %terms.1 = (f32[384,128]{1,0:T(8,128)}, f32[512,256]{1,0:T(8,128)S(1)}) custom-call(s32[1,4]{1,0:T(1,128)S(1)} %copy-done.4, s32[1,4]{1,0:T(1,128)S(1)} %copy-done.5, f32[2,256,512]{2,1,0:T(8,128)S(1)} %bitcast.21, f32[2,64,512]{2,1,0:T(8,128)S(1)} %collective-permute-done.before_ref, f32[2,64,512]{2,1,0:T(8,128)S(1)} %collective-permute-done.1.after_ref, ...), custom_call_target="tpu_custom_call" | custom-call | tf_op jit(solution)/shard_map/terms/pallas_call | solution.py:296
  11.6 0.0 copy-start.1
  11.7 7.1 %all-to-all-start = ((f32[8,48,128]{2,1,0:T(8,128)}), f32[8,48,128]{2,1,0:T(8,128)S(1)}, u32[]{:S(2)}, u32[]{:S(2)}) async-start(f32[8,48,128]{2,1,0:T(8,128)} %bitcast.8), calls=%async_computation | async-start | bytes 393216 | tf_op jit(solution)/shard_map/all_to_all | solution.py:321
  18.7 0.0 copy-done.1
  18.7 1.2 %deposit.1 = (f32[2,256,512]{2,1,0:T(8,128)S(1)}, f32[2,64,512]{2,1,0:T(8,128)S(1)}, f32[2,64,512]{2,1,0:T(8,128)S(1)}) custom-call(s32[1,4]{1,0:T(1,128)S(1)} %copy-done.4, s32[1,4]{1,0:T(1,128)S(1)} %copy-done.5, f32[2,256,512]{2,1,0:T(8,128)S(1)} %bitcast.22, f32[2,128,128]{2,1,0:T(8,128)S(1)} %copy-done.1, f32[512,256]{1,0:T(8,128)S(1)} %get-tuple-element.16.back_ref), custom_call_target="tpu_custom_call" | custom-call | tf_op jit(solution)/shard_map/deposit/pallas_call | solution.py:325
  19.9 4.9 %collective-permute-start.2 = (f32[2,64,512]{2,1,0:T(8,128)S(1)}, f32[2,64,512]{2,1,0:T(8,128)S(1)}, u32[]{:S(2)}, u32[]{:S(2)}) collective-permute-start(f32[2,64,512]{2,1,0:T(8,128)S(1)} %get-tuple-element.18), channel_id=1, source_target_pairs={{0,1},{1,2},{2,3},{4,5},{5,6},{6,7},{8,9},{9,10},{10,11},{12,13},{... | collective-permute-start | bytes 786440 | tf_op jit(solution)/shard_map/ppermute | solution.py:340
  24.8 1.3 %collective-permute-start.3 = (f32[2,64,512]{2,1,0:T(8,128)S(1)}, f32[2,64,512]{2,1,0:T(8,128)S(1)}, u32[]{:S(2)}, u32[]{:S(2)}) collective-permute-start(f32[2,64,512]{2,1,0:T(8,128)S(1)} %get-tuple-element.19), channel_id=1, source_target_pairs={{1,0},{2,1},{3,2},{5,4},{6,5},{7,6},{9,8},{10,9},{11,10},{13,12},{... | collective-permute-start | bytes 786440 | tf_op jit(solution)/shard_map/ppermute | solution.py:339
  26.1 1.1 all-to-all-done
  27.2 26.4 %all_to_all.38 = f32[16,1,384]{2,1,0:T(1,128)S(1)} all-to-all(f32[16,1,384]{2,1,0:T(1,128)S(1)} %bitcast.26), channel_id=1, replica_groups={{0,4,8,12,16,20,24,28,32,36,40,44,48,52,56,60},{64,68,72,76,80,84,88,92..., dimensions={0} | all-to-all | bytes 49152 | tf_op jit(solution)/shard_map/all_to_all | solution.py:350
  53.6 0.6 fold.1
  54.2 6.3 %all-to-all-start.2 = ((f32[4,1,512]{2,1,0:T(1,128)}), f32[4,1,512]{2,1,0:T(1,128)S(1)}, u32[]{:S(2)}, u32[]{:S(2)}) async-start(f32[4,1,512]{2,1,0:T(1,128)} %bitcast.12), calls=%async_computation.2 | async-start | bytes 16384 | tf_op jit(solution)/shard_map/all_to_all | solution.py:377
  60.5 0.0 copy-start.7
  60.5 0.7 copy-done.2
  61.2 0.0 copy-done.3
  61.2 0.0 copy-done.6
  61.2 0.5 bands.1
  61.7 0.0 collective-permute-done.2.above_ref
  61.7 0.0 collective-permute-done.3.below_ref
  61.7 1.2 %update.1 = (f32[2,256,512]{2,1,0:T(8,128)}, f32[1280,128]{1,0:T(8,128)S(1)}) custom-call(f32[2,256,512]{2,1,0:T(8,128)S(1)} %get-tuple-element.17.own_ref, f32[2,64,512]{2,1,0:T(8,128)S(1)} %collective-permute-done.2.above_ref, f32[2,64,512]{2,1,0:T(8,128)S(1)} %collective-permute-done.3.below_ref, bf16[512,256]{1,0:T(8,128)(2,1)S(1)} %get-tuple-element.20.dh_ref, ...), custom_call_target="tpu_custom_call" | custom-call | tf_op jit(solution)/shard_map/update/pallas_call | solution.py:356
  62.9 1.4 %all-to-all-done.2 = f32[4,1,512]{2,1,0:T(1,128)S(1)} async-done(((f32[4,1,512]{2,1,0:T(1,128)}), f32[4,1,512]{2,1,0:T(1,128)S(1)}, u32[]{:S(2)}, u32[]{:S(2)}) %all-to-all-start.2) | async-done | bytes 8224 | tf_op jit(solution)/shard_map/all_to_all | solution.py:377
  64.3 50.0 %all_to_all.39 = f32[128,1,1280]{2,1,0:T(1,128)S(1)} all-to-all(f32[128,1,1280]{2,1,0:T(1,128)S(1)} %bitcast.23), channel_id=1, replica_groups=mesh['angle'=128,'tile'=4] {'angle'}, dimensions={0} | all-to-all | bytes 1310720 | tf_op jit(solution)/shard_map/all_to_all | solution.py:388
  114.3 1.2 volume.1
  (7 shorter events, 0.0 us)
Async XLA Ops:
  0.6 6.7 %copy-start = (f32[2,1,256,512]{3,2,1,0:T(8,128)S(1)}, f32[2,1,256,512]{3,2,1,0:T(8,128)}, u32[]{:S(2)}) copy-start(f32[2,1,256,512]{3,2,1,0:T(8,128)} %param.11) | copy-start | bytes 3145732
  1.8 4.4 %collective-permute-start.1 = (f32[2,64,512]{2,1,0:T(8,128)S(1)}, f32[2,64,512]{2,1,0:T(8,128)S(1)}, u32[]{:S(2)}, u32[]{:S(2)}) collective-permute-start(f32[2,64,512]{2,1,0:T(8,128)S(1)} %get-tuple-element.35), channel_id=1, source_target_pairs={{1,0},{2,1},{3,2},{5,4},{6,5},{7,6},{9,8},{10,9},{11,10},{13,12},{... | collective-permute-start | bytes 786440 | tf_op jit(solution)/shard_map/ppermute | solution.py:281
  3.1 4.2 %copy-start.4 = (s32[1,4]{1,0:T(1,128)S(1)}, s32[1,4]{1,0:T(1,128)}, u32[]{:S(2)}) copy-start(s32[1,4]{1,0:T(1,128)} %row_ref.3) | copy-start | bytes 52
  3.1 4.2 %copy-start.5 = (s32[1,4]{1,0:T(1,128)S(1)}, s32[1,4]{1,0:T(1,128)}, u32[]{:S(2)}) copy-start(s32[1,4]{1,0:T(1,128)} %col_ref.3) | copy-start | bytes 52
  3.1 4.2 %collective-permute-start = (f32[2,64,512]{2,1,0:T(8,128)S(1)}, f32[2,64,512]{2,1,0:T(8,128)S(1)}, u32[]{:S(2)}, u32[]{:S(2)}) collective-permute-start(f32[2,64,512]{2,1,0:T(8,128)S(1)} %get-tuple-element.36), channel_id=1, source_target_pairs={{0,1},{1,2},{2,3},{4,5},{5,6},{6,7},{8,9},{9,10},{10,11},{12,13},{... | collective-permute-start | bytes 786440 | tf_op jit(solution)/shard_map/ppermute | solution.py:280
  11.6 7.1 %copy-start.1 = (f32[2,128,128]{2,1,0:T(8,128)S(1)}, f32[2,128,128]{2,1,0:T(8,128)}, u32[]{:S(2)}) copy-start(f32[2,128,128]{2,1,0:T(8,128)} %probe_ref.1) | copy-start | bytes 393220
  11.7 15.5 %all-to-all-start = ((f32[8,48,128]{2,1,0:T(8,128)}), f32[8,48,128]{2,1,0:T(8,128)S(1)}, u32[]{:S(2)}, u32[]{:S(2)}) async-start(f32[8,48,128]{2,1,0:T(8,128)} %bitcast.8), calls=%async_computation | async-start | bytes 393216 | tf_op jit(solution)/shard_map/all_to_all | solution.py:321
  19.9 41.8 %collective-permute-start.2 = (f32[2,64,512]{2,1,0:T(8,128)S(1)}, f32[2,64,512]{2,1,0:T(8,128)S(1)}, u32[]{:S(2)}, u32[]{:S(2)}) collective-permute-start(f32[2,64,512]{2,1,0:T(8,128)S(1)} %get-tuple-element.18), channel_id=1, source_target_pairs={{0,1},{1,2},{2,3},{4,5},{5,6},{6,7},{8,9},{9,10},{10,11},{12,13},{... | collective-permute-start | bytes 786440 | tf_op jit(solution)/shard_map/ppermute | solution.py:340
  24.8 36.9 %collective-permute-start.3 = (f32[2,64,512]{2,1,0:T(8,128)S(1)}, f32[2,64,512]{2,1,0:T(8,128)S(1)}, u32[]{:S(2)}, u32[]{:S(2)}) collective-permute-start(f32[2,64,512]{2,1,0:T(8,128)S(1)} %get-tuple-element.19), channel_id=1, source_target_pairs={{1,0},{2,1},{3,2},{5,4},{6,5},{7,6},{9,8},{10,9},{11,10},{13,12},{... | collective-permute-start | bytes 786440 | tf_op jit(solution)/shard_map/ppermute | solution.py:339
  54.2 10.1 %all-to-all-start.2 = ((f32[4,1,512]{2,1,0:T(1,128)}), f32[4,1,512]{2,1,0:T(1,128)S(1)}, u32[]{:S(2)}, u32[]{:S(2)}) async-start(f32[4,1,512]{2,1,0:T(1,128)} %bitcast.12), calls=%async_computation.2 | async-start | bytes 16384 | tf_op jit(solution)/shard_map/all_to_all | solution.py:377
  60.5 0.7 copy-start.2
  60.5 0.7 copy-start.3
  60.5 0.7 copy-start.6
  60.5 0.7 copy-start.7

commit v6 on v5

--- a/solution.py
+++ b/solution.py
@@ -185,31 +185,25 @@
 
 
 def gather_kernel(share_ref, sum_ref):
-    count = share_ref.shape[0] // sum_ref.shape[0]
-    step = sum_ref.shape[0]
-    total = share_ref[:step, :]
-    for i in range(1, count):
-        total = total + share_ref[i * step : (i + 1) * step, :]
-    sum_ref[...] = total
-
-
-def fold_kernel(share_ref, fold_ref):
+    tiles = sum_ref.shape[0] // (3 * LINE)
+    step = 3 * LINE
+    count = share_ref.shape[0] // step
+    for j in range(3):
+        total = share_ref[pl.ds(j, LINE, stride=3), :]
+        for i in range(1, count):
+            total = total + share_ref[pl.ds(i * step + j, LINE, stride=3), :]
+        for t in range(tiles):
+            sum_ref[pl.ds(3 * t + j, LINE, stride=3 * tiles), :] = total
+
+
+def line_kernel(share_ref, packed_ref, sent_ref):
+    del packed_ref
     count = share_ref.shape[0] // 3
-    fold_ref[...] = jnp.zeros(fold_ref.shape, F32)
-    for j in range(3):
-        total = jnp.sum(share_ref[pl.ds(j, count, stride=3), :], axis=0, keepdims=True)
-        for t in range(fold_ref.shape[0] // 4):
-            fold_ref[4 * t + j : 4 * t + j + 1, :] = total
-
-
-def line_kernel(fold_ref, packed_ref, sent_ref):
-    del packed_ref
-    sums = [fold_ref[j : j + 1, :] for j in range(3)]
-    for t in range(1, fold_ref.shape[0] // 4):
-        for j in range(3):
-            sums[j] = sums[j] + fold_ref[4 * t + j : 4 * t + j + 1, :]
+    sums = [
+        jnp.sum(share_ref[pl.ds(j, count, stride=3), :], axis=0, keepdims=True) for j in range(3)
+    ]
     scale = lax.rsqrt(sums[2] + EPSILON)
-    peers = fold_ref.shape[1]
+    peers = share_ref.shape[1]
     pieces = sent_ref.shape[0] // peers
     for j in range(2):
         line = jnp.broadcast_to(sums[j] * scale, (peers, peers))
@@ -273,7 +267,8 @@
 
     groups = angles // LINE
     across = [[g * LINE + i for g in range(groups)] for i in range(LINE)]
-    along = [[g * LINE + i for i in range(LINE)] for g in range(groups)]
+    block = LINE * tiles
+    along = [[g * block + i for i in range(block)] for g in range(groups)]
 
     current = projection[:, 0]
     shape = jax.ShapeDtypeStruct
@@ -341,14 +336,15 @@
 
     gathered = pl.pallas_call(
         gather_kernel,
-        out_shape=pltpu.VMEM((3 * LINE, side), F32),
+        out_shape=pltpu.VMEM((3 * block, side), F32),
         in_specs=vmem(1),
         out_specs=vmem(1)[0],
         name="gather",
         compiler_params=pltpu.CompilerParams(vmem_limit_bytes=4 << 20),
     )(held(shares))
     seconds = lax.all_to_all(
-        gathered.reshape(LINE, 3 * side), "angle", 0, 0, tiled=True, axis_index_groups=along
+        gathered.reshape(block, 3 * side), ("angle", "tile"), 0, 0,
+        tiled=True, axis_index_groups=along,
     )
 
     peers = rows // 2
@@ -366,15 +362,6 @@
         compiler_params=pltpu.CompilerParams(vmem_limit_bytes=12 << 20),
     )(held(own), held(above), held(below), held(det_high), held(det_low))
 
-    folded = pl.pallas_call(
-        fold_kernel,
-        out_shape=pltpu.VMEM((4 * tiles, side), F32),
-        in_specs=vmem(1),
-        out_specs=vmem(1)[0],
-        name="fold",
-        compiler_params=pltpu.CompilerParams(vmem_limit_bytes=4 << 20),
-    )(held(seconds.reshape(3 * LINE, side)))
-    merged = lax.all_to_all(folded.reshape(tiles, 4 * side), "tile", 0, 0, tiled=True)
     sent = pl.pallas_call(
         line_kernel,
         out_shape=pltpu.VMEM((peers * pieces, 128), F32),
@@ -383,7 +370,7 @@
         input_output_aliases={1: 0},
         name="line",
         compiler_params=pltpu.CompilerParams(vmem_limit_bytes=4 << 20),
-    )(held(merged.reshape(4 * tiles, side)), held(packed))
+    )(held(seconds.reshape(3 * block, side)), held(packed))
 
     arrived = lax.all_to_all(
         sent.reshape(peers, pieces * 128), "angle", 0, 0, tiled=True

time: 116 us -> 116 us (level)
  the two profiles are of different devices: /device:TPU:32 before, /device:TPU:1 now
where the time goes in v6:
time: 116 us; the launch traced here: 115 us
  blocking collectives  59.5 us (51%)
  starting transfers between devices  34.8 us (30%)
  waiting for transfers between devices  9.92 us (9%)
  Pallas kernels  8.41 us (7%)
  local copies, waits for them, and re-layouts  1.85 us (2%)
    all_to_all x1, blocking collectives, local(): lax.all_to_all(sent.reshape(peers, pieces * 128), 'angle', 0, 0, tiled=True)  49.8 us
    all_to_all x1, starting transfers between devices, local(): lax.all_to_all(gathered.reshape(block, 3 * side), ('angle', 'tile'), 0, 0...  18.7 us
    all_to_all x1, blocking collectives, local(): lax.all_to_all(terms, 'angle', 0, 0, tiled=True, axis_index_groups=across)  9.71 us
    ppermute x1, starting transfers between devices, local(): after = lax.ppermute(current[:, :half], 'tile', down)  8.75 us
    ppermute x1, waiting for transfers between devices, local(): below = lax.ppermute(upper, 'tile', down)  4.65 us
    pallas_call x1, Pallas kernels, local(): pl.pallas_call(terms_kernel, out_shape=(pltpu.VMEM((3 * side, side), F32)...  3.69 us
    ppermute x1, starting transfers between devices, local(): above = lax.ppermute(lower, 'tile', up)  3.54 us
    ppermute x1, waiting for transfers between devices, local(): before = lax.ppermute(current[:, rows - half:], 'tile', up)  3.28 us
  transfers between devices with their start and end apart: 5, of which 4 were waited for; matrix products, arithmetic and copies ran while one was open for 0% of the time, Pallas kernels for 3%

profile of v6, /device:TPU:1, one launch (start us, length us, event | category | flops | bytes accessed | tf_op | source)
XLA Modules:
  0.0 115.3 jit_solution(6602090601900065011)
XLA Ops:
  0.6 0.0 copy-start
  0.6 1.2 %fusion = (f32[2,64,512]{2,1,0:T(8,128)S(1)}, f32[2,64,512]{2,1,0:T(8,128)S(1)}) fusion(f32[2,256,512]{2,1,0:T(8,128)} %bitcast.18), kind=kLoop, calls=%fused_computation | loop fusion | bytes 1048576 | tf_op jit(solution)/shard_map/slice | solution.py:276
  1.8 8.7 %collective-permute-start.1 = (f32[2,64,512]{2,1,0:T(8,128)S(1)}, f32[2,64,512]{2,1,0:T(8,128)S(1)}, u32[]{:S(2)}, u32[]{:S(2)}) collective-permute-start(f32[2,64,512]{2,1,0:T(8,128)S(1)} %get-tuple-element.35), channel_id=1, source_target_pairs={{1,0},{2,1},{3,2},{5,4},{6,5},{7,6},{9,8},{10,9},{11,10},{13,12},{... | collective-permute-start | bytes 786440 | tf_op jit(solution)/shard_map/ppermute | solution.py:276
  10.6 0.0 copy-start.4
  10.6 0.0 copy-start.5
  10.6 1.9 %collective-permute-start = (f32[2,64,512]{2,1,0:T(8,128)S(1)}, f32[2,64,512]{2,1,0:T(8,128)S(1)}, u32[]{:S(2)}, u32[]{:S(2)}) collective-permute-start(f32[2,64,512]{2,1,0:T(8,128)S(1)} %get-tuple-element.36), channel_id=1, source_target_pairs={{0,1},{1,2},{2,3},{4,5},{5,6},{6,7},{8,9},{9,10},{10,11},{12,13},{... | collective-permute-start | bytes 786440 | tf_op jit(solution)/shard_map/ppermute | solution.py:275
  12.5 0.0 collective-permute-done.1.after_ref
  12.5 3.3 %collective-permute-done.before_ref = f32[2,64,512]{2,1,0:T(8,128)S(1)} collective-permute-done((f32[2,64,512]{2,1,0:T(8,128)S(1)}, f32[2,64,512]{2,1,0:T(8,128)S(1)}, u32[]{:S(2)}, u32[]{:S(2)}) %collective-permute-start) | collective-permute-done | bytes 262176 | tf_op jit(solution)/shard_map/ppermute | solution.py:275
  15.8 0.0 copy-done
  15.8 0.0 copy-done.4
  15.8 0.0 copy-done.5
  15.8 3.7 %terms.1 = (f32[384,128]{1,0:T(8,128)S(1)}, f32[512,256]{1,0:T(8,128)S(1)}) custom-call(s32[1,4]{1,0:T(1,128)S(1)} %copy-done.4, s32[1,4]{1,0:T(1,128)S(1)} %copy-done.5, f32[2,256,512]{2,1,0:T(8,128)S(1)} %bitcast.19, f32[2,64,512]{2,1,0:T(8,128)S(1)} %collective-permute-done.before_ref, f32[2,64,512]{2,1,0:T(8,128)S(1)} %collective-permute-done.1.after_ref, ...), custom_call_target="tpu_custom_call" | custom-call | tf_op jit(solution)/shard_map/terms/pallas_call | solution.py:291
  19.5 9.7 %all_to_all.29 = f32[8,48,128]{2,1,0:T(8,128)S(1)} all-to-all(f32[8,48,128]{2,1,0:T(8,128)S(1)} %bitcast.25), channel_id=1, replica_groups={{0,64,128,192,256,320,384,448},{4,68,132,196,260,324,388,452},{8,72,136..., dimensions={0} | all-to-all | bytes 393216 | tf_op jit(solution)/shard_map/all_to_all | solution.py:316
  29.2 0.7 gather.1
  29.9 18.7 %all-to-all-start.1 = ((f32[64,1,384]{2,1,0:T(1,128)}), f32[64,1,384]{2,1,0:T(1,128)S(1)}, u32[]{:S(2)}, u32[]{:S(2)}) async-start(f32[64,1,384]{2,1,0:T(1,128)} %bitcast.10), calls=%async_computation.1 | async-start | bytes 196608 | tf_op jit(solution)/shard_map/all_to_all | solution.py:345
  48.6 1.2 %deposit.1 = (f32[2,256,512]{2,1,0:T(8,128)S(1)}, f32[2,64,512]{2,1,0:T(8,128)S(1)}, f32[2,64,512]{2,1,0:T(8,128)S(1)}) custom-call(s32[1,4]{1,0:T(1,128)S(1)} %copy-done.4, s32[1,4]{1,0:T(1,128)S(1)} %copy-done.5, f32[2,256,512]{2,1,0:T(8,128)S(1)} %bitcast.20, f32[2,128,128]{2,1,0:T(8,128)S(1)} %copy-done.1, f32[512,256]{1,0:T(8,128)S(1)} %get-tuple-element.16.back_ref), custom_call_target="tpu_custom_call" | custom-call | tf_op jit(solution)/shard_map/deposit/pallas_call | solution.py:320
  49.8 3.5 %collective-permute-start.2 = (f32[2,64,512]{2,1,0:T(8,128)S(1)}, f32[2,64,512]{2,1,0:T(8,128)S(1)}, u32[]{:S(2)}, u32[]{:S(2)}) collective-permute-start(f32[2,64,512]{2,1,0:T(8,128)S(1)} %get-tuple-element.18), channel_id=1, source_target_pairs={{0,1},{1,2},{2,3},{4,5},{5,6},{6,7},{8,9},{9,10},{10,11},{12,13},{... | collective-permute-start | bytes 786440 | tf_op jit(solution)/shard_map/ppermute | solution.py:335
  53.3 0.0 copy-start.2
  53.3 1.9 %collective-permute-start.3 = (f32[2,64,512]{2,1,0:T(8,128)S(1)}, f32[2,64,512]{2,1,0:T(8,128)S(1)}, u32[]{:S(2)}, u32[]{:S(2)}) collective-permute-start(f32[2,64,512]{2,1,0:T(8,128)S(1)} %get-tuple-element.19), channel_id=1, source_target_pairs={{1,0},{2,1},{3,2},{5,4},{6,5},{7,6},{9,8},{10,9},{11,10},{13,12},{... | collective-permute-start | bytes 786440 | tf_op jit(solution)/shard_map/ppermute | solution.py:334
  55.3 0.0 copy-start.3
  55.3 0.0 copy-start.6
  55.3 0.0 copy-start.7
  55.3 0.0 copy-done.2
  55.3 0.6 copy-done.3
  55.9 0.0 copy-done.6
  56.0 0.5 bands.1
  56.5 0.5 collective-permute-done.2.above_ref
  56.9 4.6 %collective-permute-done.3.below_ref = f32[2,64,512]{2,1,0:T(8,128)S(1)} collective-permute-done((f32[2,64,512]{2,1,0:T(8,128)S(1)}, f32[2,64,512]{2,1,0:T(8,128)S(1)}, u32[]{:S(2)}, u32[]{:S(2)}) %collective-permute-start.3) | collective-permute-done | bytes 262176 | tf_op jit(solution)/shard_map/ppermute | solution.py:334
  61.6 1.2 %update.1 = (f32[2,256,512]{2,1,0:T(8,128)}, f32[1280,128]{1,0:T(8,128)S(1)}) custom-call(f32[2,256,512]{2,1,0:T(8,128)S(1)} %get-tuple-element.17.own_ref, f32[2,64,512]{2,1,0:T(8,128)S(1)} %collective-permute-done.2.above_ref, f32[2,64,512]{2,1,0:T(8,128)S(1)} %collective-permute-done.3.below_ref, bf16[512,256]{1,0:T(8,128)(2,1)S(1)} %get-tuple-element.20.dh_ref, ...), custom_call_target="tpu_custom_call" | custom-call | tf_op jit(solution)/shard_map/update/pallas_call | solution.py:352
  62.8 1.5 %all-to-all-done.1 = f32[64,1,384]{2,1,0:T(1,128)S(1)} async-done(((f32[64,1,384]{2,1,0:T(1,128)}), f32[64,1,384]{2,1,0:T(1,128)S(1)}, u32[]{:S(2)}, u32[]{:S(2)}) %all-to-all-start.1) | async-done | bytes 98336 | tf_op jit(solution)/shard_map/all_to_all | solution.py:345
  64.3 49.8 %all_to_all.30 = f32[128,1,1280]{2,1,0:T(1,128)S(1)} all-to-all(f32[128,1,1280]{2,1,0:T(1,128)S(1)} %bitcast.21), channel_id=1, replica_groups=mesh['angle'=128,'tile'=4] {'angle'}, dimensions={0} | all-to-all | bytes 1310720 | tf_op jit(solution)/shard_map/all_to_all | solution.py:375
  114.1 1.1 volume.1
  (4 shorter events, 0.0 us)
Async XLA Ops:
  0.6 15.2 %copy-start = (f32[2,1,256,512]{3,2,1,0:T(8,128)S(1)}, f32[2,1,256,512]{3,2,1,0:T(8,128)}, u32[]{:S(2)}) copy-start(f32[2,1,256,512]{3,2,1,0:T(8,128)} %param.11) | copy-start | bytes 3145732
  1.8 10.7 %collective-permute-start.1 = (f32[2,64,512]{2,1,0:T(8,128)S(1)}, f32[2,64,512]{2,1,0:T(8,128)S(1)}, u32[]{:S(2)}, u32[]{:S(2)}) collective-permute-start(f32[2,64,512]{2,1,0:T(8,128)S(1)} %get-tuple-element.35), channel_id=1, source_target_pairs={{1,0},{2,1},{3,2},{5,4},{6,5},{7,6},{9,8},{10,9},{11,10},{13,12},{... | collective-permute-start | bytes 786440 | tf_op jit(solution)/shard_map/ppermute | solution.py:276
  10.6 5.3 %copy-start.4 = (s32[1,4]{1,0:T(1,128)S(1)}, s32[1,4]{1,0:T(1,128)}, u32[]{:S(2)}) copy-start(s32[1,4]{1,0:T(1,128)} %row_ref.3) | copy-start | bytes 52
  10.6 5.2 %copy-start.5 = (s32[1,4]{1,0:T(1,128)S(1)}, s32[1,4]{1,0:T(1,128)}, u32[]{:S(2)}) copy-start(s32[1,4]{1,0:T(1,128)} %col_ref.3) | copy-start | bytes 52
  10.6 5.2 %collective-permute-start = (f32[2,64,512]{2,1,0:T(8,128)S(1)}, f32[2,64,512]{2,1,0:T(8,128)S(1)}, u32[]{:S(2)}, u32[]{:S(2)}) collective-permute-start(f32[2,64,512]{2,1,0:T(8,128)S(1)} %get-tuple-element.36), channel_id=1, source_target_pairs={{0,1},{1,2},{2,3},{4,5},{5,6},{6,7},{8,9},{9,10},{10,11},{12,13},{... | collective-permute-start | bytes 786440 | tf_op jit(solution)/shard_map/ppermute | solution.py:275
  29.9 18.7 %copy-start.1 = (f32[2,128,128]{2,1,0:T(8,128)S(1)}, f32[2,128,128]{2,1,0:T(8,128)}, u32[]{:S(2)}) copy-start(f32[2,128,128]{2,1,0:T(8,128)} %probe_ref.1) | copy-start | bytes 393220
  29.9 34.4 %all-to-all-start.1 = ((f32[64,1,384]{2,1,0:T(1,128)}), f32[64,1,384]{2,1,0:T(1,128)S(1)}, u32[]{:S(2)}, u32[]{:S(2)}) async-start(f32[64,1,384]{2,1,0:T(1,128)} %bitcast.10), calls=%async_computation.1 | async-start | bytes 196608 | tf_op jit(solution)/shard_map/all_to_all | solution.py:345
  49.8 7.2 %collective-permute-start.2 = (f32[2,64,512]{2,1,0:T(8,128)S(1)}, f32[2,64,512]{2,1,0:T(8,128)S(1)}, u32[]{:S(2)}, u32[]{:S(2)}) collective-permute-start(f32[2,64,512]{2,1,0:T(8,128)S(1)} %get-tuple-element.18), channel_id=1, source_target_pairs={{0,1},{1,2},{2,3},{4,5},{5,6},{6,7},{8,9},{9,10},{10,11},{12,13},{... | collective-permute-start | bytes 786440 | tf_op jit(solution)/shard_map/ppermute | solution.py:335
  53.3 2.0 %copy-start.2 = (f32[256,4]{0,1:T(4,128)S(1)}, f32[256,4]{0,1:T(4,128)}, u32[]{:S(2)}) copy-start(f32[256,4]{0,1:T(4,128)} %param.19) | copy-start | bytes 12292
  53.3 8.3 %collective-permute-start.3 = (f32[2,64,512]{2,1,0:T(8,128)S(1)}, f32[2,64,512]{2,1,0:T(8,128)S(1)}, u32[]{:S(2)}, u32[]{:S(2)}) collective-permute-start(f32[2,64,512]{2,1,0:T(8,128)S(1)} %get-tuple-element.19), channel_id=1, source_target_pairs={{1,0},{2,1},{3,2},{5,4},{6,5},{7,6},{9,8},{10,9},{11,10},{13,12},{... | collective-permute-start | bytes 786440 | tf_op jit(solution)/shard_map/ppermute | solution.py:334
  55.3 0.7 copy-start.3
  55.3 0.7 copy-start.6
  55.3 0.7 copy-start.7

commit v7 on v6

--- a/solution.py
+++ b/solution.py
@@ -11,6 +11,7 @@
 STEP_SIZE = 0.1
 EPSILON = 1e-06
 LINE = 16
+CORES = 2
 F32 = jnp.float32
 BF16 = jnp.bfloat16
 
@@ -131,8 +132,11 @@
         sums[0] = sums[0] + (o_re * b_re + o_im * b_im)
         sums[1] = sums[1] + (o_re * b_im - o_im * b_re)
         sums[2] = sums[2] + (o_re * o_re + o_im * o_im)
+    step = 3 * LINE
     for j in range(3):
-        term_ref[pl.ds(j, side, stride=3), :] = sums[j]
+        for i in range(term_ref.shape[0] // step):
+            first = i // CORES * LINE
+            term_ref[pl.ds(i * step + j, LINE, stride=3), :] = sums[j][first : first + LINE]
 
 
 def deposit_kernel(
@@ -266,9 +270,22 @@
     down = [(i + 1, i) for i in range(tiles - 1)]
 
     groups = angles // LINE
-    across = [[g * LINE + i for g in range(groups)] for i in range(LINE)]
-    block = LINE * tiles
-    along = [[g * block + i for i in range(block)] for g in range(groups)]
+    chips = tiles // CORES
+    block = LINE * chips
+
+    def member(g, z, chip, core):
+        return (g * LINE + z) * tiles + chip * CORES + core
+
+    across = [
+        [member(g, z, chip, core) for g in range(groups) for core in range(CORES)]
+        for z in range(LINE)
+        for chip in range(chips)
+    ]
+    along = [
+        [member(g, z, chip, core) for z in range(LINE) for chip in range(chips)]
+        for g in range(groups)
+        for core in range(CORES)
+    ]
 
     current = projection[:, 0]
     shape = jax.ShapeDtypeStruct
@@ -290,7 +307,10 @@
     here = held(current)
     terms, back = pl.pallas_call(
         terms_kernel,
-        out_shape=(pltpu.VMEM((3 * side, side), F32), pltpu.VMEM((count * side, 2 * side), F32)),
+        out_shape=(
+            pltpu.VMEM((3 * CORES * side, side), F32),
+            pltpu.VMEM((count * side, 2 * side), F32),
+        ),
         in_specs=[pl.BlockSpec(memory_space=pltpu.SMEM)] * 2
         + vmem(3)
         + [pl.BlockSpec(memory_space=pltpu.HBM)] * 4,
@@ -313,9 +333,7 @@
         stay(jnp.asarray(high)), stay(jnp.asarray(low)),
     )
 
-    shares = lax.all_to_all(
-        terms, "angle", 0, 0, tiled=True, axis_index_groups=across
-    )
+    shares = lax.all_to_all(terms, ("angle", "tile"), 0, 0, tiled=True, axis_index_groups=across)
 
     own, upper, lower = pl.pallas_call(
         deposit_kernel,

time: 116 us -> 110 us (0.948)
  the two profiles are of different devices: /device:TPU:1 before, /device:TPU:32 now
where the time goes in v7:
time: 110 us
  blocking collectives  46.1 us (42%)
  starting transfers between devices  34.9 us (32%)
  waiting for transfers between devices  16.5 us (15%)
  Pallas kernels  9.73 us (9%)
  local copies, waits for them, and re-layouts  1.86 us (2%)
    all_to_all x1, blocking collectives, local(): lax.all_to_all(sent.reshape(peers, pieces * 128), 'angle', 0, 0, tiled=True)  46.1 us
    all_to_all x1, starting transfers between devices, local(): lax.all_to_all(gathered.reshape(block, 3 * side), ('angle', 'tile'), 0, 0...  17 us
    all_to_all x1, starting transfers between devices, local(): lax.all_to_all(terms, ('angle', 'tile'), 0, 0, tiled=True, axis_index_gro...  10 us
    all_to_all x1, waiting for transfers between devices, local(): lax.all_to_all(gathered.reshape(block, 3 * side), ('angle', 'tile'), 0, 0...  9.87 us
    all_to_all x1, waiting for transfers between devices, local(): lax.all_to_all(terms, ('angle', 'tile'), 0, 0, tiled=True, axis_index_gro...  5.5 us
    pallas_call x1, Pallas kernels, local(): pl.pallas_call(terms_kernel, out_shape=(pltpu.VMEM((3 * CORES * side, sid...  4.4 us
    ppermute x1, starting transfers between devices, local(): before = lax.ppermute(current[:, rows - half:], 'tile', up)  3.05 us
    ppermute x1, starting transfers between devices, local(): above = lax.ppermute(lower, 'tile', up)  2.32 us
  transfers between devices with their start and end apart: 6, of which 3 were waited for; matrix products, arithmetic and copies ran while one was open for 0% of the time, Pallas kernels for 4%

profile of v7, /device:TPU:32, one launch (start us, length us, event | category | flops | bytes accessed | tf_op | source)
XLA Modules:
  0.0 109.9 jit_solution(8029649225216825023)
XLA Ops:
  0.6 1.2 %fusion = (f32[2,64,512]{2,1,0:T(8,128)S(1)}, f32[2,64,512]{2,1,0:T(8,128)S(1)}) fusion(f32[2,256,512]{2,1,0:T(8,128)} %bitcast.18), kind=kLoop, calls=%fused_computation | loop fusion | bytes 1048576 | tf_op jit(solution)/shard_map/slice | solution.py:293
  1.8 1.3 %collective-permute-start.1 = (f32[2,64,512]{2,1,0:T(8,128)S(1)}, f32[2,64,512]{2,1,0:T(8,128)S(1)}, u32[]{:S(2)}, u32[]{:S(2)}) collective-permute-start(f32[2,64,512]{2,1,0:T(8,128)S(1)} %get-tuple-element.35), channel_id=1, source_target_pairs={{1,0},{2,1},{3,2},{5,4},{6,5},{7,6},{9,8},{10,9},{11,10},{13,12},{... | collective-permute-start | bytes 786440 | tf_op jit(solution)/shard_map/ppermute | solution.py:293
  3.1 0.0 copy-start.4
  3.1 0.0 copy-start.5
  3.1 3.0 %collective-permute-start = (f32[2,64,512]{2,1,0:T(8,128)S(1)}, f32[2,64,512]{2,1,0:T(8,128)S(1)}, u32[]{:S(2)}, u32[]{:S(2)}) collective-permute-start(f32[2,64,512]{2,1,0:T(8,128)S(1)} %get-tuple-element.36), channel_id=1, source_target_pairs={{0,1},{1,2},{2,3},{4,5},{5,6},{6,7},{8,9},{9,10},{10,11},{12,13},{... | collective-permute-start | bytes 786440 | tf_op jit(solution)/shard_map/ppermute | solution.py:292
  6.2 0.0 collective-permute-done.1.after_ref
  6.2 1.1 %collective-permute-done.before_ref = f32[2,64,512]{2,1,0:T(8,128)S(1)} collective-permute-done((f32[2,64,512]{2,1,0:T(8,128)S(1)}, f32[2,64,512]{2,1,0:T(8,128)S(1)}, u32[]{:S(2)}, u32[]{:S(2)}) %collective-permute-start) | collective-permute-done | bytes 262176 | tf_op jit(solution)/shard_map/ppermute | solution.py:292
  7.3 0.0 copy-done.4
  7.3 4.4 %terms.1 = (f32[768,128]{1,0:T(8,128)}, f32[512,256]{1,0:T(8,128)S(1)}) custom-call(s32[1,4]{1,0:T(1,128)S(1)} %copy-done.4, s32[1,4]{1,0:T(1,128)S(1)} %copy-done.5, f32[2,256,512]{2,1,0:T(8,128)S(1)} %bitcast.19, f32[2,64,512]{2,1,0:T(8,128)S(1)} %collective-permute-done.before_ref, f32[2,64,512]{2,1,0:T(8,128)S(1)} %collective-permute-done.1.after_ref, ...), custom_call_target="tpu_custom_call" | custom-call | tf_op jit(solution)/shard_map/terms/pallas_call | solution.py:308
  11.7 0.0 copy-start.1
  11.7 10.0 %all-to-all-start = ((f32[16,48,128]{2,1,0:T(8,128)}), f32[16,48,128]{2,1,0:T(8,128)S(1)}, u32[]{:S(2)}, u32[]{:S(2)}) async-start(f32[16,48,128]{2,1,0:T(8,128)} %bitcast.8), calls=%async_computation | async-start | bytes 786432 | tf_op jit(solution)/shard_map/all_to_all | solution.py:336
  21.8 1.8 %deposit.1 = (f32[2,256,512]{2,1,0:T(8,128)S(1)}, f32[2,64,512]{2,1,0:T(8,128)S(1)}, f32[2,64,512]{2,1,0:T(8,128)}) custom-call(s32[1,4]{1,0:T(1,128)S(1)} %copy-done.4, s32[1,4]{1,0:T(1,128)S(1)} %copy-done.5, f32[2,256,512]{2,1,0:T(8,128)S(1)} %bitcast.20, f32[2,128,128]{2,1,0:T(8,128)S(1)} %copy-done.1, f32[512,256]{1,0:T(8,128)S(1)} %get-tuple-element.16.back_ref), custom_call_target="tpu_custom_call" | custom-call | tf_op jit(solution)/shard_map/deposit/pallas_call | solution.py:338
  23.6 2.3 %collective-permute-start.2 = (f32[2,64,512]{2,1,0:T(8,128)}, f32[2,64,512]{2,1,0:T(8,128)S(1)}, u32[]{:S(2)}, u32[]{:S(2)}) collective-permute-start(f32[2,64,512]{2,1,0:T(8,128)} %get-tuple-element.18), channel_id=1, source_target_pairs={{0,1},{1,2},{2,3},{4,5},{5,6},{6,7},{8,9},{9,10},{10,11},{12,13},{... | collective-permute-start | bytes 786440 | tf_op jit(solution)/shard_map/ppermute | solution.py:353
  25.9 1.3 %collective-permute-start.3 = (f32[2,64,512]{2,1,0:T(8,128)S(1)}, f32[2,64,512]{2,1,0:T(8,128)S(1)}, u32[]{:S(2)}, u32[]{:S(2)}) collective-permute-start(f32[2,64,512]{2,1,0:T(8,128)S(1)} %get-tuple-element.19), channel_id=1, source_target_pairs={{1,0},{2,1},{3,2},{5,4},{6,5},{7,6},{9,8},{10,9},{11,10},{13,12},{... | collective-permute-start | bytes 786440 | tf_op jit(solution)/shard_map/ppermute | solution.py:352
  27.2 5.5 %all-to-all-done = f32[16,48,128]{2,1,0:T(8,128)S(1)} async-done(((f32[16,48,128]{2,1,0:T(8,128)}), f32[16,48,128]{2,1,0:T(8,128)S(1)}, u32[]{:S(2)}, u32[]{:S(2)}) %all-to-all-start) | async-done | bytes 393248 | tf_op jit(solution)/shard_map/all_to_all | solution.py:336
  32.7 0.7 gather.1
  33.3 17.0 %all-to-all-start.1 = ((f32[32,1,384]{2,1,0:T(1,128)}), f32[32,1,384]{2,1,0:T(1,128)S(1)}, u32[]{:S(2)}, u32[]{:S(2)}) async-start(f32[32,1,384]{2,1,0:T(1,128)} %bitcast.10), calls=%async_computation.1 | async-start | bytes 98304 | tf_op jit(solution)/shard_map/all_to_all | solution.py:363
  50.3 0.0 copy-start.2
  50.3 0.0 copy-start.3
  50.3 0.0 copy-start.6
  50.3 0.0 copy-start.7
  50.3 0.6 copy-done.2
  51.0 0.0 copy-done.3
  51.0 0.0 copy-done.6
  51.0 0.0 copy-done.7
  51.0 0.5 bands.1
  51.5 0.0 collective-permute-done.2.above_ref
  51.5 0.0 collective-permute-done.3.below_ref
  51.6 1.2 %update.1 = (f32[2,256,512]{2,1,0:T(8,128)}, f32[1280,128]{1,0:T(8,128)S(1)}) custom-call(f32[2,256,512]{2,1,0:T(8,128)S(1)} %get-tuple-element.17.own_ref, f32[2,64,512]{2,1,0:T(8,128)S(1)} %collective-permute-done.2.above_ref, f32[2,64,512]{2,1,0:T(8,128)S(1)} %collective-permute-done.3.below_ref, bf16[512,256]{1,0:T(8,128)(2,1)S(1)} %get-tuple-element.20.dh_ref, ...), custom_call_target="tpu_custom_call" | custom-call | tf_op jit(solution)/shard_map/update/pallas_call | solution.py:370
  52.7 9.9 %all-to-all-done.1 = f32[32,1,384]{2,1,0:T(1,128)S(1)} async-done(((f32[32,1,384]{2,1,0:T(1,128)}), f32[32,1,384]{2,1,0:T(1,128)S(1)}, u32[]{:S(2)}, u32[]{:S(2)}) %all-to-all-start.1) | async-done | bytes 49184 | tf_op jit(solution)/shard_map/all_to_all | solution.py:363
  62.6 46.1 %all_to_all.29 = f32[128,1,1280]{2,1,0:T(1,128)S(1)} all-to-all(f32[128,1,1280]{2,1,0:T(1,128)S(1)} %bitcast.21), channel_id=1, replica_groups=mesh['angle'=128,'tile'=4] {'angle'}, dimensions={0} | all-to-all | bytes 1310720 | tf_op jit(solution)/shard_map/all_to_all | solution.py:393
  108.8 1.1 %volume.1 = (f32[2,2,128,256]{3,2,1,0:T(8,128)}, f32[2,128,128]{2,1,0:T(8,128)}) custom-call(f32[1280,128]{1,0:T(8,128)S(1)} %bitcast.22, bf16[128,128]{1,0:T(8,128)(2,1)S(1)} %get-tuple-element.25.ah_ref, bf16[128,128]{1,0:T(8,128)(2,1)S(1)} %get-tuple-element.26.al_ref), custom_call_target="tpu_custom_call" | custom-call | tf_op jit(solution)/shard_map/volume/pallas_call | solution.py:397
  (5 shorter events, 0.0 us)
Async XLA Ops:
  0.6 6.7 %copy-start = (f32[2,1,256,512]{3,2,1,0:T(8,128)S(1)}, f32[2,1,256,512]{3,2,1,0:T(8,128)}, u32[]{:S(2)}) copy-start(f32[2,1,256,512]{3,2,1,0:T(8,128)} %param.11) | copy-start | bytes 3145732
  1.8 4.4 %collective-permute-start.1 = (f32[2,64,512]{2,1,0:T(8,128)S(1)}, f32[2,64,512]{2,1,0:T(8,128)S(1)}, u32[]{:S(2)}, u32[]{:S(2)}) collective-permute-start(f32[2,64,512]{2,1,0:T(8,128)S(1)} %get-tuple-element.35), channel_id=1, source_target_pairs={{1,0},{2,1},{3,2},{5,4},{6,5},{7,6},{9,8},{10,9},{11,10},{13,12},{... | collective-permute-start | bytes 786440 | tf_op jit(solution)/shard_map/ppermute | solution.py:293
  3.1 4.2 %copy-start.4 = (s32[1,4]{1,0:T(1,128)S(1)}, s32[1,4]{1,0:T(1,128)}, u32[]{:S(2)}) copy-start(s32[1,4]{1,0:T(1,128)} %row_ref.3) | copy-start | bytes 52
  3.1 4.2 %copy-start.5 = (s32[1,4]{1,0:T(1,128)S(1)}, s32[1,4]{1,0:T(1,128)}, u32[]{:S(2)}) copy-start(s32[1,4]{1,0:T(1,128)} %col_ref.3) | copy-start | bytes 52
  3.1 4.2 %collective-permute-start = (f32[2,64,512]{2,1,0:T(8,128)S(1)}, f32[2,64,512]{2,1,0:T(8,128)S(1)}, u32[]{:S(2)}, u32[]{:S(2)}) collective-permute-start(f32[2,64,512]{2,1,0:T(8,128)S(1)} %get-tuple-element.36), channel_id=1, source_target_pairs={{0,1},{1,2},{2,3},{4,5},{5,6},{6,7},{8,9},{9,10},{10,11},{12,13},{... | collective-permute-start | bytes 786440 | tf_op jit(solution)/shard_map/ppermute | solution.py:292
  11.7 10.0 %copy-start.1 = (f32[2,128,128]{2,1,0:T(8,128)S(1)}, f32[2,128,128]{2,1,0:T(8,128)}, u32[]{:S(2)}) copy-start(f32[2,128,128]{2,1,0:T(8,128)} %probe_ref.1) | copy-start | bytes 393220
  11.7 20.9 %all-to-all-start = ((f32[16,48,128]{2,1,0:T(8,128)}), f32[16,48,128]{2,1,0:T(8,128)S(1)}, u32[]{:S(2)}, u32[]{:S(2)}) async-start(f32[16,48,128]{2,1,0:T(8,128)} %bitcast.8), calls=%async_computation | async-start | bytes 786432 | tf_op jit(solution)/shard_map/all_to_all | solution.py:336
  23.6 28.0 %collective-permute-start.2 = (f32[2,64,512]{2,1,0:T(8,128)}, f32[2,64,512]{2,1,0:T(8,128)S(1)}, u32[]{:S(2)}, u32[]{:S(2)}) collective-permute-start(f32[2,64,512]{2,1,0:T(8,128)} %get-tuple-element.18), channel_id=1, source_target_pairs={{0,1},{1,2},{2,3},{4,5},{5,6},{6,7},{8,9},{9,10},{10,11},{12,13},{... | collective-permute-start | bytes 786440 | tf_op jit(solution)/shard_map/ppermute | solution.py:353
  25.9 25.7 %collective-permute-start.3 = (f32[2,64,512]{2,1,0:T(8,128)S(1)}, f32[2,64,512]{2,1,0:T(8,128)S(1)}, u32[]{:S(2)}, u32[]{:S(2)}) collective-permute-start(f32[2,64,512]{2,1,0:T(8,128)S(1)} %get-tuple-element.19), channel_id=1, source_target_pairs={{1,0},{2,1},{3,2},{5,4},{6,5},{7,6},{9,8},{10,9},{11,10},{13,12},{... | collective-permute-start | bytes 786440 | tf_op jit(solution)/shard_map/ppermute | solution.py:352
  33.3 29.3 %all-to-all-start.1 = ((f32[32,1,384]{2,1,0:T(1,128)}), f32[32,1,384]{2,1,0:T(1,128)S(1)}, u32[]{:S(2)}, u32[]{:S(2)}) async-start(f32[32,1,384]{2,1,0:T(1,128)} %bitcast.10), calls=%async_computation.1 | async-start | bytes 98304 | tf_op jit(solution)/shard_map/all_to_all | solution.py:363
  50.3 0.7 copy-start.2
  50.3 0.7 copy-start.3
  50.3 0.7 copy-start.6
  50.3 0.7 copy-start.7
